TPU v7x, 32 devices: a whole 2x2x4 slice. The times are simulated.
32 devices in a mesh: seq: 8 (over y, x, core), ep: 4 (over z).
Axes of the slice: x: 2, y: 2, z: 4, core: 2. Of those that a mesh axis runs over, the one named last changes fastest.
Arguments:
- activations: bfloat16 [4096, 2880], P(('seq', 'ep')), may hold values from -6 to 6
- attn_gain: float32 [2880], replicated, may hold values from 0.1 to 1.9
- query_weight: bfloat16 [2880, 4096], P('seq', 'ep')
- key_weight: bfloat16 [2880, 512], P('seq', 'ep')
- value_weight: bfloat16 [2880, 512], P('seq', 'ep'), may hold values from -0.109375 to 0.109375
- output_weight: bfloat16 [4096, 2880], P('ep', 'seq'), may hold values from -0.375 to 0.375
- sink_logits: float32 [64], P('ep'), may hold values from 0 to 5
- mlp_gain: float32 [2880], replicated, may hold values from 0.1 to 1.9
- expert_ids: int32 [4096, 4], P(('seq', 'ep')), may hold values from 0 to 31, all different within a row; in each aligned block of 128 rows (0 to 127, 128 to 255, ...) at most 24 rows name the same one
- expert_gates: float32 [4096, 4], P(('seq', 'ep')), may hold values from 0.1 to 1
- expert_in: bfloat16 [32, 2880, 2880], P(('seq', 'ep')), may hold values from -0.109375 to 0.109375
- expert_out: bfloat16 [32, 1440, 2880], P(('seq', 'ep')), may hold values from -0.15625 to 0.15625
Outputs:
- layer_out: bfloat16 [4096, 2880], P(('seq', 'ep'))
Inputs may be any that keep to these rules, and one draw needn't show every extreme that they name: `expert_ids`: in each aligned block of 128 rows (the rows of one device) no expert is named by more than 24 rows; in some blocks one expert is named by exactly 24 rows.
All inputs are finite; a program needn't handle non-finite values.
Results may differ from a plain program's by a relative error of at most 0.014.
The roundings to bfloat16 on the way count: a program that leaves them out, or rounds other values in their place, can miss the bound.
Values may be sent and summed in bfloat16 or wider, within the bound.
A program may use at most 128 MiB of HBM per device.

v0:
```python
import functools

import jax
import jax.numpy as jnp
from jax import lax
from jax.experimental import pallas as pl
from jax.experimental.layout import Layout, with_layout_constraint
from jax.experimental.pallas import tpu as pltpu
from jax.sharding import PartitionSpec as P

MESH = pl.DeviceIdType.MESH

HD = 64
WIN = 128


def passed_along(x, axis, by):
    count = lax.axis_size(axis)
    pairs = [(i, i + by) for i in range(count) if 0 <= i + by < count]
    return lax.ppermute(x, axis, pairs)


def normed(rows_f32, gain_vec):
    inv_rms = lax.rsqrt(jnp.mean(rows_f32 * rows_f32, axis=-1, keepdims=True) + 1e-05)
    return rows_f32 * inv_rms * gain_vec


def rotate(head_vals, positions):
    half_dim = head_vals.shape[-1] // 2
    inv_freq = 150000.0 ** (-jnp.arange(half_dim, dtype=jnp.float32) / half_dim)
    angles = positions[:, None] * inv_freq[None, :]
    cosines = jnp.cos(angles)[:, None, :]
    sines = jnp.sin(angles)[:, None, :]
    first = head_vals[..., :half_dim]
    second = head_vals[..., half_dim:]
    return jnp.concatenate(
        [first * cosines - second * sines, second * cosines + first * sines], axis=-1
    )


def attend(queries, key_rows, val_rows, sink_grid, query_first, win_len):
    scores = (
        jnp.einsum("qkgd,jkd->kgqj", queries, key_rows, preferred_element_type=jnp.float32) * 0.125
    )
    q_pos = query_first + jnp.arange(queries.shape[0], dtype=jnp.int32)
    k_pos = query_first - win_len + jnp.arange(key_rows.shape[0], dtype=jnp.int32)
    offset = q_pos[:, None] - k_pos[None, :]
    allowed = (offset >= 0) & (offset < win_len) & (k_pos[None, :] >= 0)
    scores = jnp.where(allowed, scores, jnp.float32(-1e30))
    peak_val = jnp.maximum(jnp.max(scores, axis=-1), sink_grid[:, :, None])
    exp_terms = jnp.exp(scores - peak_val[..., None])
    denominator = jnp.sum(exp_terms, axis=-1) + jnp.exp(sink_grid[:, :, None] - peak_val)
    weights = (exp_terms / denominator[..., None]).astype(jnp.bfloat16)
    mixed_vals = jnp.einsum("kgqj,jkd->qkgd", weights, val_rows, preferred_element_type=jnp.float32)
    return mixed_vals.astype(jnp.bfloat16)


def remote(src, dst, send_sem, recv_sem, device):
    return pltpu.make_async_remote_copy(
        src_ref=src,
        dst_ref=dst,
        send_sem=send_sem,
        recv_sem=recv_sem,
        device_id=device,
        device_id_type=MESH,
    )


def gather_kernel(n_seq, n_ep, n_line, n_plane, *refs):
    total = n_line + n_plane
    ins, outs, bufs = refs[:total], refs[total : 2 * total], refs[2 * total : 3 * total]
    own_sem, line_send, line_recv, plane_send, plane_recv, fwd_send = refs[3 * total :]
    seq, ep = lax.axis_index("seq"), lax.axis_index("ep")
    chips = n_seq // 2
    chip, core = seq // 2, seq % 2
    partner = chip * 2 + 1 - core

    barrier = pltpu.get_barrier_semaphore()

    @pl.when(ep > 0)
    def _():
        pl.semaphore_signal(barrier, inc=1, device_id=(seq, ep - 1), device_id_type=MESH)

    @pl.when(ep < n_ep - 1)
    def _():
        pl.semaphore_signal(barrier, inc=1, device_id=(seq, ep + 1), device_id_type=MESH)

    for d in range(1, chips):
        peer = lax.rem(chip + d, chips) * 2 + core
        pl.semaphore_signal(barrier, inc=1, device_id=(peer, ep), device_id_type=MESH)
    pl.semaphore_signal(barrier, inc=1, device_id=(partner, ep), device_id_type=MESH)
    neighbours = (ep > 0).astype(jnp.int32) + (ep < n_ep - 1).astype(jnp.int32)
    pl.semaphore_wait(barrier, chips + neighbours)

    def line_copies(step, which, act):
        for i in which:
            left_src, right_src = ep - step, ep + step

            @pl.when((left_src >= 0) & (ep < n_ep - 1))
            def _():
                src = ins[i] if step == 0 else outs[i].at[left_src]
                act(
                    remote(
                        src,
                        outs[i].at[left_src],
                        line_send.at[i, 0, step],
                        line_recv.at[i, left_src],
                        (seq, ep + 1),
                    )
                )

            @pl.when((right_src < n_ep) & (ep > 0))
            def _():
                src = ins[i] if step == 0 else outs[i].at[right_src]
                act(
                    remote(
                        src,
                        outs[i].at[right_src],
                        line_send.at[i, 1, step],
                        line_recv.at[i, right_src],
                        (seq, ep - 1),
                    )
                )

    def line_arrived(step, which):
        for i in which:
            for src in (ep - step, ep + step):

                @pl.when((src >= 0) & (src < n_ep))
                def _():
                    remote(
                        ins[i],
                        outs[i].at[src],
                        line_send.at[i, 0, 0],
                        line_recv.at[i, src],
                        (seq, ep),
                    ).wait_recv()

    def plane_copy(i, d):
        peer = lax.rem(chip + d, chips) * 2 + core
        if d == 0:
            peer = partner
        return remote(
            ins[n_line + i],
            outs[n_line + i].at[seq],
            plane_send.at[i, d],
            plane_recv.at[i, seq],
            (peer, ep),
        )

    def fwd_copy(i, d):
        src = lax.rem(chip + d, chips) * 2 + core
        return remote(
            outs[n_line + i].at[src],
            outs[n_line + i].at[src],
            fwd_send.at[i, d],
            plane_recv.at[i, src],
            (partner, ep),
        )

    def plane_arrived(i, src):
        remote(
            ins[n_line + i],
            outs[n_line + i].at[src],
            plane_send.at[i, 0],
            plane_recv.at[i, src],
            (partner, ep),
        ).wait_recv()

    every = range(n_line)
    line_copies(0, every, lambda c: c.start())
    for i in range(n_plane):
        for d in range(chips):
            plane_copy(i, d).start()
    for i in range(total):
        pltpu.make_async_copy(ins[i], bufs[i], own_sem.at[i]).start()
    for i in range(total):
        pltpu.make_async_copy(ins[i], bufs[i], own_sem.at[i]).wait()
        mine = outs[i].at[ep if i < n_line else seq]
        pltpu.make_async_copy(bufs[i], mine, own_sem.at[i]).start()
    for step in range(1, n_ep - 1):
        line_arrived(step, every)
        line_copies(step, every, lambda c: c.start())
    for i in range(n_plane):
        for d in range(1, chips):
            plane_arrived(i, lax.rem(chip + d, chips) * 2 + core)
            fwd_copy(i, d).start()
    line_arrived(n_ep - 1, every)
    for i in range(n_plane):
        for d in range(chips):
            plane_arrived(i, lax.rem(chip + d, chips) * 2 + 1 - core)
    for i in range(total):
        mine = outs[i].at[ep if i < n_line else seq]
        pltpu.make_async_copy(bufs[i], mine, own_sem.at[i]).wait()
    for step in range(n_ep - 1):
        line_copies(step, every, lambda c: c.wait_send())
    for i in range(n_plane):
        for d in range(chips):
            plane_copy(i, d).wait_send()
        for d in range(1, chips):
            fwd_copy(i, d).wait_send()


def gathered(line, plane):
    n_seq, n_ep = lax.axis_size("seq"), lax.axis_size("ep")
    arrays = tuple(line) + tuple(plane)
    n_line, n_plane, chips = len(line), len(plane), n_seq // 2
    counts = [n_ep] * n_line + [n_seq] * n_plane
    anywhere = pl.BlockSpec(memory_space=pl.ANY)
    sem = pltpu.SemaphoreType.DMA
    return pl.pallas_call(
        functools.partial(gather_kernel, n_seq, n_ep, n_line, n_plane),
        out_shape=[jax.ShapeDtypeStruct((c,) + a.shape, a.dtype) for c, a in zip(counts, arrays)],
        in_specs=[anywhere] * len(arrays),
        out_specs=[anywhere] * len(arrays),
        scratch_shapes=[pltpu.VMEM(a.shape, a.dtype) for a in arrays]
        + [
            sem((len(arrays),)),
            sem((n_line, 2, n_ep)),
            sem((n_line, n_ep)),
            sem((n_plane, chips)),
            sem((n_plane, n_seq)),
            sem((n_plane, chips)),
        ],
        compiler_params=pltpu.CompilerParams(
            collective_id=0, has_side_effects=True, vmem_limit_bytes=16 << 20
        ),
        name="gather",
    )(*arrays)


def signal_all(barrier, n_seq, n_ep, seq, ep, line):
    for d in range(1, n_seq):
        pl.semaphore_signal(
            barrier, inc=1, device_id=(lax.rem(seq + d, n_seq), ep), device_id_type=MESH
        )
    count = jnp.int32(n_seq - 1)
    for d in line:
        there = (ep + d >= 0) & (ep + d < n_ep)

        @pl.when(there)
        def _():
            pl.semaphore_signal(barrier, inc=1, device_id=(seq, ep + d), device_id_type=MESH)

        count = count + there.astype(jnp.int32)
    pl.semaphore_wait(barrier, count)


def column_chunks(width, most=1024):
    return [(c, min(most, width - c)) for c in range(0, width, most)]


def dispatch_kernel(
    n_seq, n_ep, cap, x_ref, pick_ref, out_ref, held, staged, line_send, line_recv, send, recv, own
):
    seq, ep = lax.axis_index("seq"), lax.axis_index("ep")
    width = x_ref.shape[1]
    signal_all(pltpu.get_barrier_semaphore(), n_seq, n_ep, seq, ep, (-1, 1))

    def relay(step, src, away, act):
        @pl.when((src >= 0) & (src < n_ep) & (ep + away >= 0) & (ep + away < n_ep))
        def _():
            act(
                remote(
                    x_ref if step == 0 else held.at[src],
                    held.at[src],
                    line_send.at[(away + 1) // 2, step],
                    line_recv.at[src],
                    (seq, ep + away),
                )
            )

    def part(src, d):
        peer = lax.rem(seq + d, n_seq)
        return remote(
            staged.at[src, peer],
            out_ref.at[seq * n_ep + src],
            send.at[src, d],
            recv.at[seq * n_ep + src],
            (peer, ep),
        )

    def own_part(src):
        return pltpu.make_async_copy(staged.at[src, seq], out_ref.at[seq * n_ep + src], own.at[src])

    def hand_out(src, rows_ref):
        for c, size in column_chunks(width):
            picked = jnp.dot(
                pick_ref[src], rows_ref[:, c : c + size], preferred_element_type=jnp.float32
            )
            for s in range(n_seq):
                staged[src, s, :, c : c + size] = picked[s * cap : (s + 1) * cap].astype(
                    jnp.bfloat16
                )
        for d in range(1, n_seq):
            part(src, d).start()
        own_part(src).start()

    relay(0, ep, 1, lambda c: c.start())
    relay(0, ep, -1, lambda c: c.start())
    hand_out(ep, x_ref)
    for step in range(1, n_ep):
        for way in (1, -1):
            src = ep - way * step
            there = (src >= 0) & (src < n_ep)

            @pl.when(there)
            def _():
                remote(
                    x_ref, held.at[src], line_send.at[0, 0], line_recv.at[src], (seq, ep)
                ).wait_recv()

            relay(step, src, way, lambda c: c.start())
        for way in (1, -1):
            src = ep - way * step
            there = (src >= 0) & (src < n_ep)

            @pl.when(there)
            def _():
                hand_out(src, held.at[src])

    for src in range(n_ep):
        own_part(src).wait()
        for d in range(1, n_seq):
            part(src, d).wait_send()
            peer = lax.rem(seq + d, n_seq)
            remote(
                staged.at[src, 0],
                out_ref.at[peer * n_ep + src],
                send.at[src, 0],
                recv.at[peer * n_ep + src],
                (peer, ep),
            ).wait_recv()
    for step in range(n_ep):
        for way in (1, -1):
            relay(step, ep - way * step, way, lambda c: c.wait_send())


def combine_kernel(
    n_seq,
    n_ep,
    cap,
    res_ref,
    gate_ref,
    mixed_ref,
    out_ref,
    back,
    parts,
    sums,
    mine,
    send,
    recv,
    own,
    line_send,
    line_recv,
):
    seq, ep = lax.axis_index("seq"), lax.axis_index("ep")
    rows, width = mixed_ref.shape
    line = [d for d in range(1 - n_ep, n_ep) if d != 0]
    signal_all(pltpu.get_barrier_semaphore(), n_seq, n_ep, seq, ep, line)

    def part(at, d):
        peer = lax.rem(seq + d, n_seq)
        return remote(
            res_ref.at[peer * n_ep + at],
            back.at[at, seq],
            send.at[at, d],
            recv.at[at, seq],
            (peer, ep),
        )

    def own_part(at):
        return pltpu.make_async_copy(res_ref.at[seq * n_ep + at], back.at[at, seq], own.at[at])

    def line_copy(at):
        return remote(
            parts.at[at], sums.at[ep], line_send.at[at], line_recv.at[ep], (seq, at)
        )

    def each(d, act):
        at = ep + d

        @pl.when((at >= 0) & (at < n_ep))
        def _():
            act(at)

    order = sorted(range(1 - n_ep, n_ep), key=lambda d: (-abs(d), d))

    def hand_out(at):
        for d in range(1, n_seq):
            part(at, d).start()
        own_part(at).start()

    for d in order:
        each(d, hand_out)

    def gather_up(at, finish):
        own_part(at).wait()
        for d in range(1, n_seq):
            peer = lax.rem(seq + d, n_seq)
            remote(
                res_ref.at[0], back.at[at, peer], send.at[at, 0], recv.at[at, peer], (peer, ep)
            ).wait_recv()
        for c, size in column_chunks(width):
            slabs = [back[at, s, :, c : c + size].astype(jnp.float32) for s in range(n_seq)]
            taken = jnp.concatenate(slabs, axis=0).astype(jnp.bfloat16)
            three = jnp.dot(gate_ref[at], taken, preferred_element_type=jnp.float32)
            finish(c, size, three[:rows] + three[rows : 2 * rows] + three[2 * rows :])

    def pass_on(at):
        def finish(c, size, value):
            parts[at, :, c : c + size] = value.astype(jnp.bfloat16)

        gather_up(at, finish)
        line_copy(at).start()

    for d in order[:-1]:
        each(d, pass_on)

    def keep(c, size, value):
        mine[:, c : c + size] = mixed_ref[:, c : c + size] + value

    gather_up(ep, keep)

    def add(at):
        remote(
            parts.at[at], sums.at[at], line_send.at[at], line_recv.at[at], (seq, at)
        ).wait_recv()
        for c, size in column_chunks(width):
            mine[:, c : c + size] += sums[at, :, c : c + size].astype(jnp.float32)

    for d in reversed(order[:-1]):
        each(d, add)
    for c, size in column_chunks(width):
        out_ref[:, c : c + size] = mine[:, c : c + size].astype(jnp.bfloat16)
    for d in order[:-1]:
        each(d, lambda at: line_copy(at).wait_send())
    for at in range(n_ep):
        for d in range(1, n_seq):
            part(at, d).wait_send()


def dispatched(rows, picks, cap):
    n_seq, n_ep = lax.axis_size("seq"), lax.axis_size("ep")
    width = rows.shape[1]
    sem = pltpu.SemaphoreType.DMA
    vmem = pl.BlockSpec(memory_space=pltpu.VMEM)
    return pl.pallas_call(
        functools.partial(dispatch_kernel, n_seq, n_ep, cap),
        out_shape=jax.ShapeDtypeStruct((n_seq * n_ep, cap, width), jnp.bfloat16),
        in_specs=[vmem, vmem],
        out_specs=pl.BlockSpec(memory_space=pl.ANY),
        scratch_shapes=[
            pltpu.VMEM((n_ep,) + rows.shape, jnp.bfloat16),
            pltpu.VMEM((n_ep, n_seq, cap, width), jnp.bfloat16),
            sem((2, n_ep)),
            sem((n_ep,)),
            sem((n_ep, n_seq)),
            sem((n_seq * n_ep,)),
            sem((n_ep,)),
        ],
        compiler_params=pltpu.CompilerParams(
            collective_id=1, has_side_effects=True, vmem_limit_bytes=40 << 20
        ),
        name="dispatch",
    )(rows, picks)


def combined(results, gates, mixed, cap):
    n_seq, n_ep = lax.axis_size("seq"), lax.axis_size("ep")
    rows, width = mixed.shape
    sem = pltpu.SemaphoreType.DMA
    vmem = pl.BlockSpec(memory_space=pltpu.VMEM)
    return pl.pallas_call(
        functools.partial(combine_kernel, n_seq, n_ep, cap),
        out_shape=jax.ShapeDtypeStruct((rows, width), jnp.bfloat16),
        in_specs=[pl.BlockSpec(memory_space=pl.ANY), vmem, vmem],
        out_specs=vmem,
        scratch_shapes=[
            pltpu.VMEM((n_ep, n_seq, cap, width), jnp.bfloat16),
            pltpu.VMEM((n_ep, rows, width), jnp.bfloat16),
            pltpu.VMEM((n_ep, rows, width), jnp.bfloat16),
            pltpu.VMEM((rows, width), jnp.float32),
            sem((n_ep, n_seq)),
            sem((n_ep, n_seq)),
            sem((n_ep,)),
            sem((n_ep,)),
            sem((n_ep,)),
        ],
        compiler_params=pltpu.CompilerParams(
            collective_id=2, has_side_effects=True, vmem_limit_bytes=48 << 20
        ),
        name="combine",
    )(results, gates, mixed)


def slot_of(ids, capacity):
    count = ids.size
    flat = ids.reshape(-1)
    earlier = jnp.arange(count)[:, None] > jnp.arange(count)[None, :]
    same = (flat[:, None] == flat[None, :]) & earlier
    ranks = jnp.sum(same.astype(jnp.int32), axis=1)
    return (flat * capacity + ranks).reshape(ids.shape)


def three_parts(x):
    high = lax.reduce_precision(x, 8, 7)
    rest = x - high
    middle = lax.reduce_precision(rest, 8, 7)
    return high.astype(jnp.bfloat16), middle.astype(jnp.bfloat16), (rest - middle).astype(jnp.bfloat16)


def by_rows(x):
    return with_layout_constraint(x, Layout(tuple(range(x.ndim))))


def body(
    activations,
    attn_gain,
    query_weight,
    key_weight,
    value_weight,
    output_weight,
    sink_logits,
    mlp_gain,
    expert_ids,
    expert_gates,
    expert_in,
    expert_out,
):
    own_rows = activations.shape[0]
    width_dim = activations.shape[1]
    seq_count = lax.axis_size("seq")
    ep_count = lax.axis_size("ep")
    tok_rows = own_rows * ep_count
    act_f32 = activations.astype(jnp.float32)
    normed_own = normed(act_f32, attn_gain).astype(jnp.bfloat16)
    q_cols = query_weight.shape[1]
    kv_cols = key_weight.shape[1]
    experts_all = seq_count * ep_count
    top_k = expert_ids.shape[1]
    capacity = max(2, 3 * own_rows * top_k // (2 * experts_all))
    capacity = -(-capacity // 8) * 8
    out_rows = lax.all_gather(output_weight.T, "seq", axis=0, tiled=True)
    (normed_all, line_slots, line_gates, *shard_rows) = gathered(
        (normed_own, slot_of(expert_ids, capacity).T, expert_gates.T),
        (query_weight, key_weight, value_weight),
    )
    normed_all = normed_all.reshape(tok_rows, width_dim)
    shard_rows = [rows.reshape(width_dim, -1) for rows in shard_rows]
    q_lin, k_lin, v_lin = tuple(
        (
            jnp.dot(normed_all, weight_rows, preferred_element_type=jnp.float32)
            for weight_rows in shard_rows
        )
    )
    q_lin, k_lin = by_rows(q_lin), by_rows(k_lin)
    first_pos = lax.axis_index("seq") * tok_rows
    positions = (first_pos + jnp.arange(tok_rows, dtype=jnp.int32)).astype(jnp.float32)
    q_heads = q_cols // HD
    kv_heads = kv_cols // HD
    group_size = q_heads // kv_heads
    queries = (
        rotate(q_lin.reshape(tok_rows, q_heads, HD), positions)
        .astype(jnp.bfloat16)
        .reshape(tok_rows, kv_heads, group_size, HD)
    )
    keys_rot = (
        rotate(k_lin.reshape(tok_rows, kv_heads, HD), positions)
        .astype(jnp.bfloat16)
        .reshape(tok_rows, kv_cols)
    )
    values_cast = v_lin.astype(jnp.bfloat16)
    prev_keys, prev_values = passed_along(
        (keys_rot[tok_rows - WIN :], values_cast[tok_rows - WIN :]), "seq", 1
    )
    key_all = jnp.concatenate([prev_keys, keys_rot], axis=0).reshape(WIN + tok_rows, kv_heads, HD)
    val_all = jnp.concatenate([prev_values, values_cast], axis=0).reshape(
        WIN + tok_rows, kv_heads, HD
    )
    block_len = min(tok_rows, 512)
    sink_grid = sink_logits.reshape(kv_heads, group_size)

    def one_block(block):
        row_first = block * block_len
        return attend(queries, key_all, val_all, sink_grid, first_pos + row_first, WIN)

    attended = lax.map(one_block, jnp.arange(tok_rows // block_len, dtype=jnp.int32)).reshape(
        tok_rows, q_cols
    )
    head_partial = lax.dot_general(
        attended, out_rows, (((1,), (1,)), ((), ())), preferred_element_type=jnp.float32
    ).astype(jnp.bfloat16)
    head_sum = lax.psum_scatter(
        by_rows(head_partial), "ep", scatter_dimension=0, tiled=True
    ).astype(jnp.float32)
    mixed = act_f32 + head_sum
    mlp_in = normed(mixed, mlp_gain).astype(jnp.bfloat16)
    plane_rows = seq_count * capacity
    place = jnp.arange(plane_rows, dtype=jnp.int32)
    first_slots = (place // capacity * ep_count + lax.axis_index("ep")) * capacity
    plane_slots = first_slots + place % capacity
    picks = sum(
        (line_slots[:, k, None, :] == plane_slots[None, :, None]).astype(jnp.bfloat16)
        for k in range(top_k)
    )
    gate_at = sum(
        jnp.where(
            line_slots[:, k, :, None] == plane_slots[None, None, :],
            line_gates[:, k, :, None],
            0.0,
        )
        for k in range(top_k)
    )
    gate_parts = jnp.concatenate(three_parts(gate_at), axis=1)
    gate_up = expert_in[0]
    down_proj = expert_out[0]
    hidden_units = down_proj.shape[0]
    arrived = dispatched(mlp_in, picks, capacity)
    lead_shape = arrived.shape[:2]
    flat_rows = arrived.reshape(-1, width_dim)
    joined = jnp.dot(flat_rows, gate_up, preferred_element_type=jnp.float32)
    gate_part = joined[:, :hidden_units]
    up_part = joined[:, hidden_units:]
    activated = ((up_part + 1.0) * gate_part * jax.nn.sigmoid(1.702 * gate_part)).astype(
        jnp.bfloat16
    )
    results = jnp.dot(activated, down_proj, preferred_element_type=jnp.float32).astype(jnp.bfloat16)
    processed = results.reshape(lead_shape + (width_dim,))
    return combined(processed, gate_parts, mixed, capacity)


def solution(mesh):
    return jax.shard_map(
        body,
        mesh=mesh,
        in_specs=(
            P(("seq", "ep"), None),
            P(),
            P("seq", "ep"),
            P("seq", "ep"),
            P("seq", "ep"),
            P("ep", "seq"),
            P("ep"),
            P(),
            P(("seq", "ep"), None),
            P(("seq", "ep"), None),
            P(("seq", "ep"), None, None),
            P(("seq", "ep"), None, None),
        ),
        out_specs=P(("seq", "ep"), None),
        check_vma=False,
    )
```

profile of v0, /device:TPU:13, one launch (start us, length us, event | category | flops | bytes accessed | tf_op | source)
XLA Modules:
  0.0 378.1 jit_solution(1963299298323251698)
XLA Ops:
  7.3 1.5 copy.33
  11.1 0.9 fusion.18.refs_0_
  12.1 1.1 copy-done
  13.2 62.5 %gather.1 = (bf16[4,128,2880]{2,1,0:T(8,128)(2,1)S(1)}, s32[4,4,128]{2,1,0:T(4,128)S(1)}, f32[4,4,128]{2,1,0:T(4,128)S(1)}, bf16[8,360,1024]{2,1,0:T(8,128)(2,1)...) custom-call(bf16[128,2880]{1,0:T(8,128)(2,1)S(1)} %fusion.18.refs_0_, ...), custom_call_target="tpu_custom_call" | custom-call | tf_op jit(solution)/shard_map/gather/pallas_call | solution.py:211
  75.7 0.9 copy-done.1
  76.6 2.6 copy-done.5
  79.2 0.9 convolution_convert_fusion.1
  80.1 3.8 collective-permute-start
  84.2 2.2 fusion.49
  86.6 2.5 collective-permute-start.1
  89.1 5.5 %fusion.50 = f32[512,1024]{0,1:T(8,128)S(1)} fusion(bf16[512,2880]{1,0:T(8,128)(2,1)S(1)} %bitcast.71, bf16[2880,1024]{1,0:T(8,128)(2,1)} %bitcast.74), kind=kOutput, calls=%fused_computation.95 | convolution fusion | flops 3019898880 | bytes 10944512 | tf_op jit(solution)/shard_map/layout_constraint | solution.py:514
  96.4 3.2 fusion.3
  99.6 4.5 %fusion = f32[2,8,512]{2,1,0:T(8,128)S(1)} fusion(f32[2,640,512,8]{2,1,3,0:T(8,128)S(1)} %get-tuple-element.58, f32[2,8,512]{2,1,0:T(8,128)S(1)} %broadcast_maximum_fusion, pred[512,640]{0,1:T(8,128)(4,1)S(1)} %fusion.21), kind=kLoop, calls=%fused_computation.3 | loop fusion | flops 20963328 | bytes 21364736 | tf_op jit(solution)/shard_map/while/body/eval_jaxpr/reduce_sum | solution.py:52
  104.2 5.9 %fusion.19 = bf16[2,64,8,512]{3,1,2,0:T(8,128)(2,1)S(1)} fusion(bf16[640,2,64,1]{0,2,3,1:T(8,128)(2,1)S(1)} %bitcast.82, f32[2,640,512,8]{2,1,3,0:T(8,128)S(1)} %get-tuple-element.58, f32[2,8,512]{2,1,0:T(8,128)S(1)} %exponential_add_fusion, f32[2,8,512]{2,1,0:T(8,128)S(1)} %broadcast_maximum_fusion, pred[512,640]{0,1:T(8,128)(4,1)S(1)} %fusion.21), kind=kOutput, calls=%fused_computation.28 | convolution fusion | flops 697827328 | bytes 22577152 | tf_op jit(solution)/shard_map/while/body/eval_jaxpr/kgqj,jkd->qkgd/dot_general | solution.py:54
  110.2 7.7 %convolution_convert_fusion = bf16[512,2880]{1,0:T(8,128)(2,1)} fusion(bf16[512,1024]{0,1:T(8,128)(2,1)S(1)} %bitcast.97, bf16[2880,1024]{1,0:T(8,128)(2,1)} %all-gather.2.cloned.1.call-done), kind=kOutput, calls=%fused_computation.11 | convolution fusion | flops 3021373440 | bytes 9895936 | tf_op jit(solution)/shard_map/dot_general | solution.py:591
  119.1 56.5 %reduce-scatter.2.cloned.1.call-done = bf16[128,2880]{1,0:T(8,128)(2,1)} async-done(((bf16[512,2880]{1,0:T(8,128)(2,1)}), bf16[128,2880]{1,0:T(8,128)(2,1)}) %reduce-scatter.2.cloned.1.call-update) | async-done | bytes 737296 | tf_op jit(solution)/shard_map/reduce_scatter | solution.py:594
  175.6 1.4 convert_add_fusion
  177.1 1.4 multiply_convert_fusion.x_ref
  178.5 60.1 %dispatch.1 = bf16[32,24,2880]{2,1,0:T(8,128)(2,1)S(1)} custom-call(bf16[128,2880]{1,0:T(8,128)(2,1)S(1)} %multiply_convert_fusion.x_ref, bf16[4,192,128]{2,1,0:T(8,128)(2,1)S(1)} %fusion.30.pick_ref), custom_call_target="tpu_custom_call" | custom-call | tf_op jit(solution)/shard_map/dispatch/pallas_call | solution.py:448
  238.6 20.1 %fusion.1 = f32[768,2880]{0,1:T(8,128)} fusion(bf16[768,2880]{1,0:T(8,128)(2,1)S(1)} %bitcast.68, bf16[1,2880,2880]{2,1,0:T(8,128)(2,1)} %param.22), kind=kOutput, calls=%fused_computation.4 | convolution fusion | flops 12740198400 | bytes 29859840 | tf_op jit(solution)/shard_map/dot_general | solution.py:622
  258.6 14.6 %fusion.7 = bf16[768,2880]{0,1:T(8,128)(2,1)} fusion(bf16[1,1440,2880]{2,1,0:T(8,128)(2,1)} %param.23, f32[768,2880]{0,1:T(8,128)} %fusion.1), kind=kOutput, calls=%fused_computation.10 | convolution fusion | flops 6381158400 | bytes 21565440 | tf_op jit(solution)/shard_map/dot_general | solution.py:628
  273.2 6.5 %copy.40 = bf16[768,2880]{1,0:T(8,128)(2,1)} copy(bf16[768,2880]{0,1:T(8,128)(2,1)} %fusion.7) | data formatting | bytes 8847360 | tf_op jit(solution)/shard_map/convert_element_type | solution.py:628
  279.7 90.4 %combine.1 = bf16[128,2880]{1,0:T(8,128)(2,1)S(1)} custom-call(bf16[32,24,2880]{2,1,0:T(8,128)(2,1)} %bitcast.76, bf16[4,384,192]{2,1,0:T(8,128)(2,1)S(1)} %pad_maximum_fusion.gate_ref, f32[128,2880]{1,0:T(8,128)S(1)} %get-tuple-element.40.mixed_ref), custom_call_target="tpu_custom_call" | custom-call | tf_op jit(solution)/shard_map/combine/pallas_call | solution.py:474
  370.1 1.1 copy.41
  (53 shorter events, 6.5 us)
Async XLA Ops:
  6.5 5.5 %copy-start.4 = (f32[128,4]{0,1:T(4,128)S(1)}, f32[128,4]{0,1:T(4,128)}, u32[]{:S(2)}) copy-start(f32[128,4]{0,1:T(4,128)} %param.21) | copy-start | bytes 6148
  6.5 5.5 %copy-start.2 = (bf16[360,128]{1,0:T(8,128)(2,1)S(1)}, bf16[360,128]{1,0:T(8,128)(2,1)}, u32[]{:S(2)}) copy-start(bf16[360,128]{1,0:T(8,128)(2,1)} %refs_4_.1) | copy-start | bytes 276484
  6.5 5.5 %copy-start.3 = (bf16[360,128]{1,0:T(8,128)(2,1)S(1)}, bf16[360,128]{1,0:T(8,128)(2,1)}, u32[]{:S(2)}) copy-start(bf16[360,128]{1,0:T(8,128)(2,1)} %refs_5_.1) | copy-start | bytes 276484
  6.5 103.6 %all-gather.2.cloned.1.call-start = ((), (), s32[]{:S(2)}) async-start(), calls=%async_computation.1 | async-start | bytes 6635520 | tf_op jit(solution)/shard_map/all_gather | solution.py:544
  7.3 168.3 %reduce-scatter.2.cloned.1.call-start = ((), (), s32[]{:S(2)}) async-start(), calls=%async_computation.2 | async-start | bytes 3768320 | tf_op jit(solution)/shard_map/reduce_scatter | solution.py:594
  8.8 3.3 copy-start.6
  12.1 1.1 copy-start
  75.7 0.9 copy-start.1
  76.6 2.6 copy-start.5
  80.1 16.1 %collective-permute-start = (bf16[128,128]{1,0:T(8,128)(2,1)S(1)}, bf16[128,128]{1,0:T(8,128)(2,1)S(1)}, u32[]{:S(2)}, u32[]{:S(2)}) collective-permute-start(bf16[128,128]{1,0:T(8,128)(2,1)S(1)} %slice.72), channel_id=1, source_target_pairs={{0,4},{4,8},{8,12},{12,16},{16,20},{20,24},{24,28},{1,5},{5,9},{9,... | collective-permute-start | bytes 98312 | tf_op jit(solution)/shard_map/ppermute | solution.py:20
  86.6 9.8 %collective-permute-start.1 = (bf16[128,128]{0,1:T(8,128)(2,1)S(1)}, bf16[128,128]{0,1:T(8,128)(2,1)S(1)}, u32[]{:S(2)}, u32[]{:S(2)}) collective-permute-start(bf16[128,128]{0,1:T(8,128)(2,1)S(1)} %bitcast.83), channel_id=1, source_target_pairs={{0,4},{4,8},{8,12},{12,16},{16,20},{20,24},{24,28},{1,5},{5,9},{9,... | collective-permute-start | bytes 98312 | tf_op jit(solution)/shard_map/ppermute | solution.py:20
  117.9 57.7 %copy-start.7 = (bf16[128,2880]{1,0:T(8,128)(2,1)S(1)}, bf16[128,2880]{1,0:T(8,128)(2,1)}, u32[]{:S(2)}) copy-start(bf16[128,2880]{1,0:T(8,128)(2,1)} %copy-done.6) | copy-start | bytes 2211844
  117.9 59.2 %copy-start.8 = (f32[2880]{0:T(1024)S(1)}, f32[2880]{0:T(1024)}, u32[]{:S(2)}) copy-start(f32[2880]{0:T(1024)} %param.19) | copy-start | bytes 34564
Sparse Core Ops, SparseCore 0:
  9.2 72.7 all-gather.1
  118.0 57.5 reduce-scatter.1
where the time goes:
time: 379 us; the launch traced here: 378 us
  Pallas kernels  213 us (56%)
  matrix products  60.1 us (16%)
  waiting for transfers between devices  57.3 us (15%)
  local copies, waits for them, and re-layouts  15.7 us (4%)
  between operations  13.7 us (4%)
  other arithmetic  12 us (3%)
  starting transfers between devices  6.34 us (2%)
    pallas_call x1, Pallas kernels, combined(): pl.pallas_call(functools.partial(combine_kernel, n_seq, n_ep, cap), out_s...  90.4 us
    pallas_call x1, Pallas kernels, gathered(): pl.pallas_call(functools.partial(gather_kernel, n_seq, n_ep, n_line, n_pl...  62.5 us
    pallas_call x1, Pallas kernels, dispatched(): pl.pallas_call(functools.partial(dispatch_kernel, n_seq, n_ep, cap), out_...  60.1 us
    reduce_scatter x1, waiting for transfers between devices, body(): lax.psum_scatter(by_rows(head_partial), 'ep', scatter_dimension=0, tiled=...  56.5 us
    dot_general x1, matrix products, body(): joined = jnp.dot(flat_rows, gate_up, preferred_element_type=jnp.float32)  20.1 us
    dot_general x1, matrix products, body(): jnp.dot(activated, down_proj, preferred_element_type=jnp.float32)  14.6 us
    another operation x2, matrix products, by_rows(): return with_layout_constraint(x, Layout(tuple(range(x.ndim))))  7.79 us
    dot_general x1, matrix products, body(): lax.dot_general(attended, out_rows, (((1,), (1,)), ((), ())), preferred_e...  7.71 us
  transfers between devices with their start and end apart: 4, of which 1 were waited for; matrix products, arithmetic and copies ran while one was open for 8% of the time, Pallas kernels for 17%

commit v1 on v0

--- a/solution.py
+++ b/solution.py
@@ -250,17 +250,63 @@
     return [(c, min(most, width - c)) for c in range(0, width, most)]
 
 
-def dispatch_kernel(
-    n_seq, n_ep, cap, x_ref, pick_ref, out_ref, held, staged, line_send, line_recv, send, recv, own
+def moe_kernel(
+    n_seq,
+    n_ep,
+    cap,
+    x_ref,
+    pick_ref,
+    gate_ref,
+    mixed_ref,
+    win_hbm,
+    wout_hbm,
+    out_ref,
+    held,
+    staged,
+    arrived,
+    back,
+    sums,
+    mine,
+    taken,
+    joined,
+    act,
+    w_in,
+    w_out,
+    weight_sem,
+    line_send,
+    line_recv,
+    send,
+    recv,
+    own,
+    back_send,
+    back_recv,
+    back_own,
+    sum_send,
+    sum_recv,
 ):
     seq, ep = lax.axis_index("seq"), lax.axis_index("ep")
-    width = x_ref.shape[1]
-    signal_all(pltpu.get_barrier_semaphore(), n_seq, n_ep, seq, ep, (-1, 1))
-
-    def relay(step, src, away, act):
+    rows, width = mixed_ref.shape
+    slots = n_seq * cap
+    hidden = wout_hbm.shape[0]
+    far = [d for d in range(1 - n_ep, n_ep) if d != 0]
+    in_copy = pltpu.make_async_copy(win_hbm, w_in, weight_sem.at[0])
+    out_copy = pltpu.make_async_copy(wout_hbm, w_out, weight_sem.at[1])
+    in_copy.start()
+    out_copy.start()
+    signal_all(pltpu.get_barrier_semaphore(), n_seq, n_ep, seq, ep, far)
+
+    def spread(buffer, c, size, value):
+        for s in range(n_seq):
+            buffer[s, :, pl.ds(c, size)] = value[s * cap : (s + 1) * cap].astype(jnp.bfloat16)
+
+    def together(buffer, c, size, first, count):
+        slabs = [buffer[first + s, :, c : c + size].astype(jnp.float32) for s in range(count)]
+        return jnp.concatenate(slabs, axis=0).astype(jnp.bfloat16)
+
+    def relay(step, src, away, act_on):
         @pl.when((src >= 0) & (src < n_ep) & (ep + away >= 0) & (ep + away < n_ep))
         def _():
-            act(
+            act_on(
                 remote(
                     x_ref if step == 0 else held.at[src],
                     held.at[src],
@@ -274,27 +320,134 @@
         peer = lax.rem(seq + d, n_seq)
         return remote(
             staged.at[src, peer],
-            out_ref.at[seq * n_ep + src],
+            arrived.at[src, seq],
             send.at[src, d],
-            recv.at[seq * n_ep + src],
+            recv.at[src, seq],
             (peer, ep),
         )
 
     def own_part(src):
-        return pltpu.make_async_copy(staged.at[src, seq], out_ref.at[seq * n_ep + src], own.at[src])
+        return pltpu.make_async_copy(
+            staged.at[src, seq], arrived.at[src, seq], own.at[src]
+        )
+
+    def back_part(src, d):
+        peer = lax.rem(seq + d, n_seq)
+        return remote(
+            staged.at[src, peer],
+            back.at[src, seq],
+            back_send.at[src, d],
+            back_recv.at[src, seq],
+            (peer, ep),
+        )
+
+    def back_own_part(src):
+        return pltpu.make_async_copy(
+            staged.at[src, seq], back.at[src, seq], back_own.at[src]
+        )
+
+    def sum_copy(at):
+        return remote(held.at[at], sums.at[ep], sum_send.at[at], sum_recv.at[ep], (seq, at))
+
+    def each(d, act_on):
+        at = ep + d
+
+        @pl.when((at >= 0) & (at < n_ep))
+        def _():
+            act_on(at)
 
     def hand_out(src, rows_ref):
         for c, size in column_chunks(width):
             picked = jnp.dot(
                 pick_ref[src], rows_ref[:, c : c + size], preferred_element_type=jnp.float32
             )
-            for s in range(n_seq):
-                staged[src, s, :, c : c + size] = picked[s * cap : (s + 1) * cap].astype(
-                    jnp.bfloat16
-                )
+            spread(staged.at[src], c, size, picked)
         for d in range(1, n_seq):
             part(src, d).start()
         own_part(src).start()
+
+    def expert(src):
+        own_part(src).wait()
+        for d in range(1, n_seq):
+            peer = lax.rem(seq + d, n_seq)
+            remote(
+                staged.at[src, seq],
+                arrived.at[src, peer],
+                send.at[src, 0],
+                recv.at[src, peer],
+                (peer, ep),
+            ).wait_recv()
+
+        group = n_seq if slots % 16 else 2
+        for s in range(0, n_seq, group):
+            taken[s * cap : (s + group) * cap, :] = together(arrived.at[src], 0, width, s, group)
+
+        def up_columns(c, size):
+            joined[:, pl.ds(c, size)] = jnp.dot(
+                taken[...], w_in[:, pl.ds(c, size)], preferred_element_type=jnp.float32
+            )
+
+        @pl.loop(0, width // 512)
+        def _(i):
+            up_columns(pl.multiple_of(i * 512, 512), 512)
+
+        if width % 512:
+            up_columns(width // 512 * 512, width % 512)
+
+        @pl.loop(0, slots // 16)
+        def _(i):
+            r = pl.ds(pl.multiple_of(i * 16, 16), 16)
+            gate = joined[r, 0:hidden]
+            up = joined[r, hidden : 2 * hidden]
+            act[r, :] = ((up + 1.0) * gate * jax.nn.sigmoid(1.702 * gate)).astype(jnp.bfloat16)
+
+        for d in range(1, n_seq):
+            part(src, d).wait_send()
+
+        def down_columns(c, size):
+            value = jnp.dot(
+                act[...], w_out[:, pl.ds(c, size)], preferred_element_type=jnp.float32
+            )
+            spread(staged.at[src], c, size, value)
+
+        @pl.loop(0, width // 512)
+        def _(i):
+            down_columns(pl.multiple_of(i * 512, 512), 512)
+
+        if width % 512:
+            down_columns(width // 512 * 512, width % 512)
+        for d in range(1, n_seq):
+            back_part(src, d).start()
+        back_own_part(src).start()
+
+    def gather_up(at, finish):
+        back_own_part(at).wait()
+        for d in range(1, n_seq):
+            peer = lax.rem(seq + d, n_seq)
+            remote(
+                staged.at[at, seq],
+                back.at[at, peer],
+                back_send.at[at, 0],
+                back_recv.at[at, peer],
+                (peer, ep),
+            ).wait_recv()
+        for c, size in column_chunks(width):
+            results = together(back.at[at], c, size, 0, n_seq)
+            three = jnp.dot(gate_ref[at], results, preferred_element_type=jnp.float32)
+            finish(c, size, three[:rows] + three[rows : 2 * rows] + three[2 * rows :])
+
+    def pass_on(step, way):
+        at = ep + way * step
+
+        @pl.when((at >= 0) & (at < n_ep))
+        def _():
+            relay(step, at, -way, lambda c: c.wait_send())
+
+            def finish(c, size, value):
+                held[at, :, c : c + size] = value.astype(jnp.bfloat16)
+
+            gather_up(at, finish)
+            sum_copy(at).start()
 
     relay(0, ep, 1, lambda c: c.start())
     relay(0, ep, -1, lambda c: c.start())
@@ -302,9 +455,8 @@
     for step in range(1, n_ep):
         for way in (1, -1):
             src = ep - way * step
-            there = (src >= 0) & (src < n_ep)
-
-            @pl.when(there)
+
+            @pl.when((src >= 0) & (src < n_ep))
             def _():
                 remote(
                     x_ref, held.at[src], line_send.at[0, 0], line_recv.at[src], (seq, ep)
@@ -312,175 +464,80 @@
 
             relay(step, src, way, lambda c: c.start())
         for way in (1, -1):
-            src = ep - way * step
-            there = (src >= 0) & (src < n_ep)
-
-            @pl.when(there)
-            def _():
-                hand_out(src, held.at[src])
-
-    for src in range(n_ep):
-        own_part(src).wait()
-        for d in range(1, n_seq):
-            part(src, d).wait_send()
-            peer = lax.rem(seq + d, n_seq)
-            remote(
-                staged.at[src, 0],
-                out_ref.at[peer * n_ep + src],
-                send.at[src, 0],
-                recv.at[peer * n_ep + src],
-                (peer, ep),
-            ).wait_recv()
-    for step in range(n_ep):
+            each(-way * step, lambda at: hand_out(at, held.at[at]))
+        if step == 1:
+            in_copy.wait()
+            out_copy.wait()
+            expert(ep)
+        else:
+            for way in (1, -1):
+                each(-way * (step - 1), expert)
+            if step > 2:
+                for way in (1, -1):
+                    pass_on(step - 2, way)
+    for way in (1, -1):
+        each(-way * (n_ep - 1), expert)
+    if n_ep > 2:
         for way in (1, -1):
-            relay(step, ep - way * step, way, lambda c: c.wait_send())
-
-
-def combine_kernel(
-    n_seq,
-    n_ep,
-    cap,
-    res_ref,
-    gate_ref,
-    mixed_ref,
-    out_ref,
-    back,
-    parts,
-    sums,
-    mine,
-    send,
-    recv,
-    own,
-    line_send,
-    line_recv,
-):
-    seq, ep = lax.axis_index("seq"), lax.axis_index("ep")
-    rows, width = mixed_ref.shape
-    line = [d for d in range(1 - n_ep, n_ep) if d != 0]
-    signal_all(pltpu.get_barrier_semaphore(), n_seq, n_ep, seq, ep, line)
-
-    def part(at, d):
-        peer = lax.rem(seq + d, n_seq)
-        return remote(
-            res_ref.at[peer * n_ep + at],
-            back.at[at, seq],
-            send.at[at, d],
-            recv.at[at, seq],
-            (peer, ep),
-        )
-
-    def own_part(at):
-        return pltpu.make_async_copy(res_ref.at[seq * n_ep + at], back.at[at, seq], own.at[at])
-
-    def line_copy(at):
-        return remote(
-            parts.at[at], sums.at[ep], line_send.at[at], line_recv.at[ep], (seq, at)
-        )
-
-    def each(d, act):
-        at = ep + d
-
-        @pl.when((at >= 0) & (at < n_ep))
-        def _():
-            act(at)
-
-    order = sorted(range(1 - n_ep, n_ep), key=lambda d: (-abs(d), d))
-
-    def hand_out(at):
-        for d in range(1, n_seq):
-            part(at, d).start()
-        own_part(at).start()
-
-    for d in order:
-        each(d, hand_out)
-
-    def gather_up(at, finish):
-        own_part(at).wait()
-        for d in range(1, n_seq):
-            peer = lax.rem(seq + d, n_seq)
-            remote(
-                res_ref.at[0], back.at[at, peer], send.at[at, 0], recv.at[at, peer], (peer, ep)
-            ).wait_recv()
-        for c, size in column_chunks(width):
-            slabs = [back[at, s, :, c : c + size].astype(jnp.float32) for s in range(n_seq)]
-            taken = jnp.concatenate(slabs, axis=0).astype(jnp.bfloat16)
-            three = jnp.dot(gate_ref[at], taken, preferred_element_type=jnp.float32)
-            finish(c, size, three[:rows] + three[rows : 2 * rows] + three[2 * rows :])
-
-    def pass_on(at):
-        def finish(c, size, value):
-            parts[at, :, c : c + size] = value.astype(jnp.bfloat16)
-
-        gather_up(at, finish)
-        line_copy(at).start()
-
-    for d in order[:-1]:
-        each(d, pass_on)
+            pass_on(n_ep - 2, way)
 
     def keep(c, size, value):
         mine[:, c : c + size] = mixed_ref[:, c : c + size] + value
 
     gather_up(ep, keep)
+    for way in (1, -1):
+        pass_on(n_ep - 1, way)
 
     def add(at):
-        remote(
-            parts.at[at], sums.at[at], line_send.at[at], line_recv.at[at], (seq, at)
-        ).wait_recv()
+        remote(held.at[at], sums.at[at], sum_send.at[at], sum_recv.at[at], (seq, at)).wait_recv()
         for c, size in column_chunks(width):
             mine[:, c : c + size] += sums[at, :, c : c + size].astype(jnp.float32)
 
-    for d in reversed(order[:-1]):
+    order = sorted(far, key=lambda d: (abs(d), d))
+    for d in order:
         each(d, add)
     for c, size in column_chunks(width):
         out_ref[:, c : c + size] = mine[:, c : c + size].astype(jnp.bfloat16)
-    for d in order[:-1]:
-        each(d, lambda at: line_copy(at).wait_send())
-    for at in range(n_ep):
+    for d in order:
+        each(d, lambda at: sum_copy(at).wait_send())
+    for way in (1, -1):
+        relay(0, ep, way, lambda c: c.wait_send())
+    for src in range(n_ep):
         for d in range(1, n_seq):
-            part(at, d).wait_send()
-
-
-def dispatched(rows, picks, cap):
+            back_part(src, d).wait_send()
+
+
+def mixture(rows_in, picks, gates, mixed, w_in, w_out, cap):
     n_seq, n_ep = lax.axis_size("seq"), lax.axis_size("ep")
-    width = rows.shape[1]
+    rows, width = mixed.shape
+    hidden = w_out.shape[0]
+    slots = n_seq * cap
     sem = pltpu.SemaphoreType.DMA
     vmem = pl.BlockSpec(memory_space=pltpu.VMEM)
+    anywhere = pl.BlockSpec(memory_space=pl.ANY)
     return pl.pallas_call(
-        functools.partial(dispatch_kernel, n_seq, n_ep, cap),
-        out_shape=jax.ShapeDtypeStruct((n_seq * n_ep, cap, width), jnp.bfloat16),
-        in_specs=[vmem, vmem],
-        out_specs=pl.BlockSpec(memory_space=pl.ANY),
+        functools.partial(moe_kernel, n_seq, n_ep, cap),
+        out_shape=jax.ShapeDtypeStruct((rows, width), jnp.bfloat16),
+        in_specs=[vmem, vmem, vmem, vmem, anywhere, anywhere],
+        out_specs=vmem,
         scratch_shapes=[
-            pltpu.VMEM((n_ep,) + rows.shape, jnp.bfloat16),
+            pltpu.VMEM((n_ep, rows, width), jnp.bfloat16),
             pltpu.VMEM((n_ep, n_seq, cap, width), jnp.bfloat16),
+            pltpu.VMEM((n_ep, n_seq, cap, width), jnp.bfloat16),
+            pltpu.VMEM((n_ep, n_seq, cap, width), jnp.bfloat16),
+            pltpu.VMEM((n_ep, rows, width), jnp.bfloat16),
+            pltpu.VMEM((rows, width), jnp.float32),
+            pltpu.VMEM((slots, width), jnp.bfloat16),
+            pltpu.VMEM((slots, width), jnp.float32),
+            pltpu.VMEM((slots, hidden), jnp.bfloat16),
+            pltpu.VMEM(w_in.shape, jnp.bfloat16),
+            pltpu.VMEM(w_out.shape, jnp.bfloat16),
+            sem((2,)),
             sem((2, n_ep)),
             sem((n_ep,)),
             sem((n_ep, n_seq)),
-            sem((n_seq * n_ep,)),
+            sem((n_ep, n_seq)),
             sem((n_ep,)),
-        ],
-        compiler_params=pltpu.CompilerParams(
-            collective_id=1, has_side_effects=True, vmem_limit_bytes=40 << 20
-        ),
-        name="dispatch",
-    )(rows, picks)
-
-
-def combined(results, gates, mixed, cap):
-    n_seq, n_ep = lax.axis_size("seq"), lax.axis_size("ep")
-    rows, width = mixed.shape
-    sem = pltpu.SemaphoreType.DMA
-    vmem = pl.BlockSpec(memory_space=pltpu.VMEM)
-    return pl.pallas_call(
-        functools.partial(combine_kernel, n_seq, n_ep, cap),
-        out_shape=jax.ShapeDtypeStruct((rows, width), jnp.bfloat16),
-        in_specs=[pl.BlockSpec(memory_space=pl.ANY), vmem, vmem],
-        out_specs=vmem,
-        scratch_shapes=[
-            pltpu.VMEM((n_ep, n_seq, cap, width), jnp.bfloat16),
-            pltpu.VMEM((n_ep, rows, width), jnp.bfloat16),
-            pltpu.VMEM((n_ep, rows, width), jnp.bfloat16),
-            pltpu.VMEM((rows, width), jnp.float32),
             sem((n_ep, n_seq)),
             sem((n_ep, n_seq)),
             sem((n_ep,)),
@@ -488,10 +545,10 @@
             sem((n_ep,)),
         ],
         compiler_params=pltpu.CompilerParams(
-            collective_id=2, has_side_effects=True, vmem_limit_bytes=48 << 20
+            collective_id=1, has_side_effects=True, vmem_limit_bytes=64000 << 10
         ),
-        name="combine",
-    )(results, gates, mixed)
+        name="mixture",
+    )(rows_in, picks, gates, mixed, w_in, w_out)
 
 
 def slot_of(ids, capacity):
@@ -613,21 +670,9 @@
         for k in range(top_k)
     )
     gate_parts = jnp.concatenate(three_parts(gate_at), axis=1)
-    gate_up = expert_in[0]
-    down_proj = expert_out[0]
-    hidden_units = down_proj.shape[0]
-    arrived = dispatched(mlp_in, picks, capacity)
-    lead_shape = arrived.shape[:2]
-    flat_rows = arrived.reshape(-1, width_dim)
-    joined = jnp.dot(flat_rows, gate_up, preferred_element_type=jnp.float32)
-    gate_part = joined[:, :hidden_units]
-    up_part = joined[:, hidden_units:]
-    activated = ((up_part + 1.0) * gate_part * jax.nn.sigmoid(1.702 * gate_part)).astype(
-        jnp.bfloat16
-    )
-    results = jnp.dot(activated, down_proj, preferred_element_type=jnp.float32).astype(jnp.bfloat16)
-    processed = results.reshape(lead_shape + (width_dim,))
-    return combined(processed, gate_parts, mixed, capacity)
+    return mixture(
+        mlp_in, picks, gate_parts, mixed, expert_in[0], expert_out[0], capacity
+    )
 
 
 def solution(mesh):

time: 379 us -> 360 us (0.950)
  the two profiles are of different devices: /device:TPU:13 before, /device:TPU:0 now
where the time goes in v1:
time: 360 us; the launch traced here: 356 us
  Pallas kernels  230 us (64%)
  waiting for transfers between devices  57.7 us (16%)
  matrix products  25.5 us (7%)
  between operations  14.2 us (4%)
  other arithmetic  13 us (4%)
  local copies, waits for them, and re-layouts  9.64 us (3%)
  starting transfers between devices  5.73 us (2%)
    pallas_call x1, Pallas kernels, mixture(): pl.pallas_call(functools.partial(moe_kernel, n_seq, n_ep, cap), out_shape...  167 us
    pallas_call x1, Pallas kernels, gathered(): pl.pallas_call(functools.partial(gather_kernel, n_seq, n_ep, n_line, n_pl...  63.2 us
    reduce_scatter x1, waiting for transfers between devices, body(): lax.psum_scatter(by_rows(head_partial), 'ep', scatter_dimension=0, tiled=...  57 us
    another operation x2, matrix products, by_rows(): return with_layout_constraint(x, Layout(tuple(range(x.ndim))))  7.79 us
    dot_general x1, matrix products, body(): lax.dot_general(attended, out_rows, (((1,), (1,)), ((), ())), preferred_e...  7.7 us
  transfers between devices with their start and end apart: 4, of which 1 were waited for; matrix products, arithmetic and copies ran while one was open for 8% of the time, Pallas kernels for 18%

profile of v1, /device:TPU:0, one launch (start us, length us, event | category | flops | bytes accessed | tf_op | source)
XLA Modules:
  0.0 356.1 jit_solution(8446101481436160368)
XLA Ops:
  6.6 0.7 all-gather.2.cloned.1.call-update
  7.3 1.5 copy.31
  8.8 0.8 copy.32
  10.8 1.1 copy-done
  11.9 63.2 %gather.1 = (bf16[4,128,2880]{2,1,0:T(8,128)(2,1)S(1)}, s32[4,4,128]{2,1,0:T(4,128)S(1)}, f32[4,4,128]{2,1,0:T(4,128)S(1)}, bf16[8,360,1024]{2,1,0:T(8,128)(2,1)...) custom-call(bf16[128,2880]{1,0:T(8,128)(2,1)S(1)} %fusion.5.refs_0_, ...), custom_call_target="tpu_custom_call" | custom-call | tf_op jit(solution)/shard_map/gather/pallas_call | solution.py:211
  75.1 0.9 copy-done.1
  76.0 2.6 copy-done.5
  78.5 0.9 convolution_convert_fusion.1
  79.5 2.3 collective-permute-start
  82.2 2.2 fusion.34
  84.5 3.3 collective-permute-start.1
  87.8 5.5 %fusion.35 = f32[512,1024]{0,1:T(8,128)S(1)} fusion(bf16[512,2880]{1,0:T(8,128)(2,1)S(1)} %bitcast.61, bf16[2880,1024]{1,0:T(8,128)(2,1)} %bitcast.64), kind=kOutput, calls=%fused_computation.82 | convolution fusion | flops 3019898880 | bytes 10944512 | tf_op jit(solution)/shard_map/layout_constraint | solution.py:571
  94.5 3.2 fusion.1
  97.7 4.5 %fusion = f32[2,8,512]{2,1,0:T(8,128)S(1)} fusion(f32[2,640,512,8]{2,1,3,0:T(8,128)S(1)} %get-tuple-element.58, f32[2,8,512]{2,1,0:T(8,128)S(1)} %broadcast_maximum_fusion, pred[512,640]{0,1:T(8,128)(4,1)S(1)} %fusion.8), kind=kLoop, calls=%fused_computation.3 | loop fusion | flops 20963328 | bytes 21364736 | tf_op jit(solution)/shard_map/while/body/eval_jaxpr/reduce_sum | solution.py:52
  102.3 5.9 %fusion.6 = bf16[2,64,8,512]{3,1,2,0:T(8,128)(2,1)S(1)} fusion(bf16[640,2,64,1]{0,2,3,1:T(8,128)(2,1)S(1)} %bitcast.73, f32[2,640,512,8]{2,1,3,0:T(8,128)S(1)} %get-tuple-element.58, f32[2,8,512]{2,1,0:T(8,128)S(1)} %exponential_add_fusion, f32[2,8,512]{2,1,0:T(8,128)S(1)} %broadcast_maximum_fusion, pred[512,640]{0,1:T(8,128)(4,1)S(1)} %fusion.8), kind=kOutput, calls=%fused_computation.17 | convolution fusion | flops 697827328 | bytes 22577152 | tf_op jit(solution)/shard_map/while/body/eval_jaxpr/kgqj,jkd->qkgd/dot_general | solution.py:54
  108.3 7.7 %convolution_convert_fusion = bf16[512,2880]{1,0:T(8,128)(2,1)} fusion(bf16[512,1024]{0,1:T(8,128)(2,1)S(1)} %bitcast.88, bf16[2880,1024]{1,0:T(8,128)(2,1)} %all-gather.2.cloned.1.call-done), kind=kOutput, calls=%fused_computation.6 | convolution fusion | flops 3021373440 | bytes 9895936 | tf_op jit(solution)/shard_map/dot_general | solution.py:648
  116.1 0.7 reduce-precision_convert_fusion.1
  116.8 1.0 pad_maximum_fusion.gate_ref
  117.8 0.9 fusion.17.pick_ref
  118.7 57.0 %reduce-scatter.2.cloned.1.call-done = bf16[128,2880]{1,0:T(8,128)(2,1)} async-done(((bf16[512,2880]{1,0:T(8,128)(2,1)}), bf16[128,2880]{1,0:T(8,128)(2,1)}) %reduce-scatter.2.cloned.1.call-update) | async-done | bytes 737296 | tf_op jit(solution)/shard_map/reduce_scatter | solution.py:651
  175.7 2.6 convert_add_fusion
  178.3 1.2 multiply_convert_fusion.x_ref
  179.5 167.1 %mixture.1 = bf16[128,2880]{1,0:T(8,128)(2,1)} custom-call(bf16[128,2880]{1,0:T(8,128)(2,1)} %multiply_convert_fusion.x_ref, bf16[4,192,128]{2,1,0:T(8,128)(2,1)} %fusion.17.pick_ref, bf16[4,384,192]{2,1,0:T(8,128)(2,1)} %pad_maximum_fusion.gate_ref, f32[128,2880]{1,0:T(8,128)} %get-tuple-element.40.mixed_ref, bf16[2880,2880]{1,0:T(8,128)(2,1)} %bitcast.66, ...), custom_call_target="tpu_custom_call" | custom-call | tf_op jit(solution)/shard_map/mixture/pallas_call | solution.py:518
  346.5 2.3 copy.38
  (57 shorter events, 2.8 us)
Async XLA Ops:
  6.5 3.9 %copy-start.11 = (s32[128,4]{0,1:T(4,128)S(1)}, s32[128,4]{0,1:T(4,128)}, u32[]{:S(2)}) copy-start(s32[128,4]{0,1:T(4,128)} %param.20) | copy-start | bytes 6148
  6.5 3.9 %copy-start.9 = (f32[2880]{0:T(1024)S(1)}, f32[2880]{0:T(1024)}, u32[]{:S(2)}) copy-start(f32[2880]{0:T(1024)} %param.13) | copy-start | bytes 34564
  6.5 4.2 %copy-start.4 = (f32[128,4]{0,1:T(4,128)S(1)}, f32[128,4]{0,1:T(4,128)}, u32[]{:S(2)}) copy-start(f32[128,4]{0,1:T(4,128)} %param.21) | copy-start | bytes 6148
  6.5 4.2 %copy-start.2 = (bf16[360,128]{1,0:T(8,128)(2,1)S(1)}, bf16[360,128]{1,0:T(8,128)(2,1)}, u32[]{:S(2)}) copy-start(bf16[360,128]{1,0:T(8,128)(2,1)} %refs_4_.1) | copy-start | bytes 276484
  6.5 4.2 %copy-start.3 = (bf16[360,128]{1,0:T(8,128)(2,1)S(1)}, bf16[360,128]{1,0:T(8,128)(2,1)}, u32[]{:S(2)}) copy-start(bf16[360,128]{1,0:T(8,128)(2,1)} %refs_5_.1) | copy-start | bytes 276484
  6.5 101.7 %all-gather.2.cloned.1.call-start = ((), (), s32[]{:S(2)}) async-start(), calls=%async_computation.1 | async-start | bytes 6635520 | tf_op jit(solution)/shard_map/all_gather | solution.py:601
  7.3 168.4 %reduce-scatter.2.cloned.1.call-start = ((), (), s32[]{:S(2)}) async-start(), calls=%async_computation.2 | async-start | bytes 3768320 | tf_op jit(solution)/shard_map/reduce_scatter | solution.py:651
  8.8 1.9 copy-start.6
  10.7 1.1 copy-start
  75.1 0.9 copy-start.1
  76.0 2.6 copy-start.5
  79.5 14.8 %collective-permute-start = (bf16[128,128]{1,0:T(8,128)(2,1)S(1)}, bf16[128,128]{1,0:T(8,128)(2,1)S(1)}, u32[]{:S(2)}, u32[]{:S(2)}) collective-permute-start(bf16[128,128]{1,0:T(8,128)(2,1)S(1)} %slice.64), channel_id=1, source_target_pairs={{0,4},{4,8},{8,12},{12,16},{16,20},{20,24},{24,28},{1,5},{5,9},{9,... | collective-permute-start | bytes 98312 | tf_op jit(solution)/shard_map/ppermute | solution.py:20
  84.5 10.0 %collective-permute-start.1 = (bf16[128,128]{0,1:T(8,128)(2,1)S(1)}, bf16[128,128]{0,1:T(8,128)(2,1)S(1)}, u32[]{:S(2)}, u32[]{:S(2)}) collective-permute-start(bf16[128,128]{0,1:T(8,128)(2,1)S(1)} %bitcast.74), channel_id=1, source_target_pairs={{0,4},{4,8},{8,12},{12,16},{16,20},{20,24},{24,28},{1,5},{5,9},{9,... | collective-permute-start | bytes 98312 | tf_op jit(solution)/shard_map/ppermute | solution.py:20
  93.4 0.8 copy-start.12
  116.0 59.7 %copy-start.7 = (bf16[128,2880]{1,0:T(8,128)(2,1)S(1)}, bf16[128,2880]{1,0:T(8,128)(2,1)}, u32[]{:S(2)}) copy-start(bf16[128,2880]{1,0:T(8,128)(2,1)} %copy-done.6) | copy-start | bytes 2211844
  116.0 62.3 %copy-start.10 = (f32[2880]{0:T(1024)S(1)}, f32[2880]{0:T(1024)}, u32[]{:S(2)}) copy-start(f32[2880]{0:T(1024)} %param.19) | copy-start | bytes 34564
  175.7 2.6 copy-start.8
Sparse Core Ops, SparseCore 0:
  9.3 72.5 all-gather.1
  116.1 59.5 reduce-scatter.1

commit v2 on v1

--- a/solution.py
+++ b/solution.py
@@ -288,12 +288,11 @@
     rows, width = mixed_ref.shape
     slots = n_seq * cap
     hidden = wout_hbm.shape[0]
-    far = [d for d in range(1 - n_ep, n_ep) if d != 0]
     in_copy = pltpu.make_async_copy(win_hbm, w_in, weight_sem.at[0])
     out_copy = pltpu.make_async_copy(wout_hbm, w_out, weight_sem.at[1])
     in_copy.start()
     out_copy.start()
-    signal_all(pltpu.get_barrier_semaphore(), n_seq, n_ep, seq, ep, far)
+    signal_all(pltpu.get_barrier_semaphore(), n_seq, n_ep, seq, ep, (-1, 1))
 
     def spread(buffer, c, size, value):
         for s in range(n_seq):
@@ -346,8 +345,24 @@
             staged.at[src, seq], back.at[src, seq], back_own.at[src]
         )
 
-    def sum_copy(at):
-        return remote(held.at[at], sums.at[ep], sum_send.at[at], sum_recv.at[ep], (seq, at))
+    def landing(at, step, way):
+        return jnp.where(way == -1, n_ep, at) if step == 1 else at
+
+    def sum_copy(at, step, way, i):
+        c, size = column_chunks(width)[i]
+        slot = landing(at, step, way)
+        return remote(
+            held.at[at, :, c : c + size],
+            sums.at[slot, :, c : c + size],
+            sum_send.at[at, i],
+            sum_recv.at[slot, i],
+            (seq, ep + way),
+        )
+
+    def sum_arrived(slot, i):
+        c, size = column_chunks(width)[i]
+        piece = sums.at[slot, :, c : c + size]
+        remote(piece, piece, sum_send.at[0, 0], sum_recv.at[slot, i], (seq, ep)).wait_recv()
 
     def each(d, act_on):
         at = ep + d
@@ -431,10 +446,10 @@
                 back_recv.at[at, peer],
                 (peer, ep),
             ).wait_recv()
-        for c, size in column_chunks(width):
+        for i, (c, size) in enumerate(column_chunks(width)):
             results = together(back.at[at], c, size, 0, n_seq)
             three = jnp.dot(gate_ref[at], results, preferred_element_type=jnp.float32)
-            finish(c, size, three[:rows] + three[rows : 2 * rows] + three[2 * rows :])
+            finish(i, c, size, three[:rows] + three[rows : 2 * rows] + three[2 * rows :])
 
     def pass_on(step, way):
         at = ep + way * step
@@ -443,11 +458,23 @@
         def _():
             relay(step, at, -way, lambda c: c.wait_send())
 
-            def finish(c, size, value):
-                held[at, :, c : c + size] = value.astype(jnp.bfloat16)
+            def finish(i, c, size, value):
+                before = ep - way
+                joins = (before >= 0) & (before < n_ep)
+
+                @pl.when(joins)
+                def _():
+                    sum_arrived(at, i)
+                    sofar = sums[at, :, c : c + size].astype(jnp.float32)
+                    held[at, :, c : c + size] = (value + sofar).astype(jnp.bfloat16)
+
+                @pl.when(jnp.logical_not(joins))
+                def _():
+                    held[at, :, c : c + size] = value.astype(jnp.bfloat16)
+
+                sum_copy(at, step, way, i).start()
 
             gather_up(at, finish)
-            sum_copy(at).start()
 
     relay(0, ep, 1, lambda c: c.start())
     relay(0, ep, -1, lambda c: c.start())
@@ -472,34 +499,56 @@
         else:
             for way in (1, -1):
                 each(-way * (step - 1), expert)
-            if step > 2:
-                for way in (1, -1):
-                    pass_on(step - 2, way)
+    toward = jnp.where(2 * ep < n_ep, 1, -1)
+    at_end = (ep == 0) | (ep == n_ep - 1)
+
+    @pl.when(at_end)
+    def _():
+        for step in range(1, n_ep - 2):
+            pass_on(step, toward)
+
     for way in (1, -1):
         each(-way * (n_ep - 1), expert)
-    if n_ep > 2:
-        for way in (1, -1):
-            pass_on(n_ep - 2, way)
-
-    def keep(c, size, value):
+
+    @pl.when(jnp.logical_not(at_end))
+    def _():
+        for step in range(1, n_ep - 2):
+            pass_on(step, toward)
+
+    for step in range(max(1, n_ep - 2), n_ep):
+        pass_on(step, toward)
+
+    def keep(i, c, size, value):
         mine[:, c : c + size] = mixed_ref[:, c : c + size] + value
 
     gather_up(ep, keep)
-    for way in (1, -1):
-        pass_on(n_ep - 1, way)
-
-    def add(at):
-        remote(held.at[at], sums.at[at], sum_send.at[at], sum_recv.at[at], (seq, at)).wait_recv()
-        for c, size in column_chunks(width):
-            mine[:, c : c + size] += sums[at, :, c : c + size].astype(jnp.float32)
-
-    order = sorted(far, key=lambda d: (abs(d), d))
-    for d in order:
-        each(d, add)
+
+    for step in range(1, n_ep // 2):
+        pass_on(step, -toward)
+
+    def add(slot):
+        for i, (c, size) in enumerate(column_chunks(width)):
+            sum_arrived(slot, i)
+            mine[:, c : c + size] += sums[slot, :, c : c + size].astype(jnp.float32)
+
+    @pl.when(ep > 0)
+    def _():
+        add(ep)
+
+    @pl.when(ep < n_ep - 1)
+    def _():
+        add(n_ep)
+
     for c, size in column_chunks(width):
         out_ref[:, c : c + size] = mine[:, c : c + size].astype(jnp.bfloat16)
-    for d in order:
-        each(d, lambda at: sum_copy(at).wait_send())
+    for step in range(1, n_ep):
+        for way in (1, -1):
+
+            def sent(at):
+                for i in range(len(column_chunks(width))):
+                    sum_copy(at, step, way, i).wait_send()
+
+            each(way * step, sent)
     for way in (1, -1):
         relay(0, ep, way, lambda c: c.wait_send())
     for src in range(n_ep):
@@ -525,7 +574,7 @@
             pltpu.VMEM((n_ep, n_seq, cap, width), jnp.bfloat16),
             pltpu.VMEM((n_ep, n_seq, cap, width), jnp.bfloat16),
             pltpu.VMEM((n_ep, n_seq, cap, width), jnp.bfloat16),
-            pltpu.VMEM((n_ep, rows, width), jnp.bfloat16),
+            pltpu.VMEM((n_ep + 1, rows, width), jnp.bfloat16),
             pltpu.VMEM((rows, width), jnp.float32),
             pltpu.VMEM((slots, width), jnp.bfloat16),
             pltpu.VMEM((slots, width), jnp.float32),
@@ -541,8 +590,8 @@
             sem((n_ep, n_seq)),
             sem((n_ep, n_seq)),
             sem((n_ep,)),
-            sem((n_ep,)),
-            sem((n_ep,)),
+            sem((n_ep, len(column_chunks(width)))),
+            sem((n_ep + 1, len(column_chunks(width)))),
         ],
         compiler_params=pltpu.CompilerParams(
             collective_id=1, has_side_effects=True, vmem_limit_bytes=64000 << 10
@@ -598,11 +647,12 @@
     top_k = expert_ids.shape[1]
     capacity = max(2, 3 * own_rows * top_k // (2 * experts_all))
     capacity = -(-capacity // 8) * 8
-    out_rows = lax.all_gather(output_weight.T, "seq", axis=0, tiled=True)
     (normed_all, line_slots, line_gates, *shard_rows) = gathered(
         (normed_own, slot_of(expert_ids, capacity).T, expert_gates.T),
         (query_weight, key_weight, value_weight),
     )
+    normed_all, out_cols = lax.optimization_barrier((normed_all, output_weight.T))
+    out_rows = lax.all_gather(out_cols, "seq", axis=0, tiled=True)
     normed_all = normed_all.reshape(tok_rows, width_dim)
     shard_rows = [rows.reshape(width_dim, -1) for rows in shard_rows]
     q_lin, k_lin, v_lin = tuple(

time: 360 us -> 351 us (0.975)
  Pallas kernels: 230 us -> 208 us
  waiting for transfers between devices: 57.7 us -> 68.1 us
    pallas_call x1, Pallas kernels: 167 us -> 151 us  [mixture(): pl.pallas_call(functools.partial(moe_kernel, n_seq, n_ep, cap), out_shape...]
    all_gather x1, waiting for transfers between devices: 0.02 us -> 12.5 us  [body(): out_rows = lax.all_gather(out_cols, 'seq', axis=0, tiled=True)]
    pallas_call x1, Pallas kernels: 63.2 us -> 57.6 us  [gathered(): pl.pallas_call(functools.partial(gather_kernel, n_seq, n_ep, n_line, n_pl...]
    unnamed x28 -> x26, local copies, waits for them, and re-layouts: 6.84 us -> 7.77 us
  transfers between devices with their start and end apart: 4 -> 4, of which waited for: 1 -> 2; matrix products, arithmetic and copies ran while one was open for 8% -> 8% of each run, Pallas kernels for 18% -> 0%
where the time goes in v2:
time: 351 us; the launch traced here: 347 us
  Pallas kernels  208 us (59%)
  waiting for transfers between devices  68.1 us (19%)
  matrix products  26.6 us (8%)
  other arithmetic  14.4 us (4%)
  between operations  14.2 us (4%)
  local copies, waits for them, and re-layouts  10.6 us (3%)
  starting transfers between devices  4.75 us (1%)
    pallas_call x1, Pallas kernels, mixture(): pl.pallas_call(functools.partial(moe_kernel, n_seq, n_ep, cap), out_shape...  151 us
    pallas_call x1, Pallas kernels, gathered(): pl.pallas_call(functools.partial(gather_kernel, n_seq, n_ep, n_line, n_pl...  57.6 us
    reduce_scatter x1, waiting for transfers between devices, body(): lax.psum_scatter(by_rows(head_partial), 'ep', scatter_dimension=0, tiled=...  55.6 us
    all_gather x1, waiting for transfers between devices, body(): out_rows = lax.all_gather(out_cols, 'seq', axis=0, tiled=True)  12.5 us
    another operation x2, matrix products, by_rows(): return with_layout_constraint(x, Layout(tuple(range(x.ndim))))  7.8 us
    unnamed x26, local copies, waits for them, and re-layouts  7.77 us
    dot_general x1, matrix products, body(): lax.dot_general(attended, out_rows, (((1,), (1,)), ((), ())), preferred_e...  7.69 us
  transfers between devices with their start and end apart: 4, of which 2 were waited for; matrix products, arithmetic and copies ran while one was open for 8% of the time, Pallas kernels for 0%

profile of v2, /device:TPU:0, one launch (start us, length us, event | category | flops | bytes accessed | tf_op | source)
XLA Modules:
  0.0 346.8 jit_solution(9104961979682830901)
XLA Ops:
  6.5 1.5 copy.31
  10.3 0.9 fusion.5.refs_0_
  11.4 1.1 copy-done
  12.5 57.6 %gather.1 = (bf16[4,128,2880]{2,1,0:T(8,128)(2,1)S(1)}, s32[4,4,128]{2,1,0:T(4,128)S(1)}, f32[4,4,128]{2,1,0:T(4,128)S(1)}, bf16[8,360,1024]{2,1,0:T(8,128)(2,1)...) custom-call(bf16[128,2880]{1,0:T(8,128)(2,1)S(1)} %fusion.5.refs_0_, ...), custom_call_target="tpu_custom_call" | custom-call | tf_op jit(solution)/shard_map/gather/pallas_call | solution.py:211
  70.1 0.9 copy-done.1
  71.0 2.5 copy-done.5
  73.5 0.9 copy-done.6
  74.5 2.1 convolution_convert_fusion.1
  76.6 1.3 collective-permute-start
  78.2 2.3 fusion.34
  80.5 3.4 collective-permute-start.1
  84.0 5.5 %fusion.35 = f32[512,1024]{0,1:T(8,128)S(1)} fusion(bf16[512,2880]{1,0:T(8,128)(2,1)S(1)} %bitcast.61, bf16[2880,1024]{1,0:T(8,128)(2,1)} %bitcast.64), kind=kOutput, calls=%fused_computation.82 | convolution fusion | flops 3019898880 | bytes 10944512 | tf_op jit(solution)/shard_map/layout_constraint | solution.py:620
  90.6 3.2 fusion.1
  93.9 4.5 %fusion = f32[2,8,512]{2,1,0:T(8,128)S(1)} fusion(f32[2,640,512,8]{2,1,3,0:T(8,128)S(1)} %get-tuple-element.62, f32[2,8,512]{2,1,0:T(8,128)S(1)} %broadcast_maximum_fusion, pred[512,640]{0,1:T(8,128)(4,1)S(1)} %fusion.8), kind=kLoop, calls=%fused_computation.3 | loop fusion | flops 20963328 | bytes 21364736 | tf_op jit(solution)/shard_map/while/body/eval_jaxpr/reduce_sum | solution.py:52
  98.5 5.9 %fusion.6 = bf16[2,64,8,512]{3,1,2,0:T(8,128)(2,1)S(1)} fusion(bf16[640,2,64,1]{0,2,3,1:T(8,128)(2,1)S(1)} %bitcast.73, f32[2,640,512,8]{2,1,3,0:T(8,128)S(1)} %get-tuple-element.62, f32[2,8,512]{2,1,0:T(8,128)S(1)} %exponential_add_fusion, f32[2,8,512]{2,1,0:T(8,128)S(1)} %broadcast_maximum_fusion, pred[512,640]{0,1:T(8,128)(4,1)S(1)} %fusion.8), kind=kOutput, calls=%fused_computation.17 | convolution fusion | flops 697827328 | bytes 22577152 | tf_op jit(solution)/shard_map/while/body/eval_jaxpr/kgqj,jkd->qkgd/dot_general | solution.py:54
  104.4 12.5 %all-gather.2.cloned.1.call-done = bf16[2880,1024]{1,0:T(8,128)(2,1)} async-done(((bf16[360,1024]{1,0:T(8,128)(2,1)}), bf16[2880,1024]{1,0:T(8,128)(2,1)}) %all-gather.2.cloned.1.call-update) | async-done | bytes 5898256 | tf_op jit(solution)/shard_map/all_gather | solution.py:655
  116.8 7.7 %convolution_convert_fusion = bf16[512,2880]{1,0:T(8,128)(2,1)} fusion(bf16[512,1024]{0,1:T(8,128)(2,1)S(1)} %bitcast.88, bf16[2880,1024]{1,0:T(8,128)(2,1)} %all-gather.2.cloned.1.call-done), kind=kOutput, calls=%fused_computation.6 | convolution fusion | flops 3021373440 | bytes 9895936 | tf_op jit(solution)/shard_map/dot_general | solution.py:698
  125.4 1.0 pad_maximum_fusion.gate_ref
  126.4 0.9 fusion.17.pick_ref
  127.3 55.6 %reduce-scatter.2.cloned.1.call-done = bf16[128,2880]{1,0:T(8,128)(2,1)} async-done(((bf16[512,2880]{1,0:T(8,128)(2,1)}), bf16[128,2880]{1,0:T(8,128)(2,1)}) %reduce-scatter.2.cloned.1.call-update) | async-done | bytes 737296 | tf_op jit(solution)/shard_map/reduce_scatter | solution.py:701
  182.9 2.6 convert_add_fusion
  185.5 1.2 multiply_convert_fusion.x_ref
  186.7 150.6 %mixture.1 = bf16[128,2880]{1,0:T(8,128)(2,1)} custom-call(bf16[128,2880]{1,0:T(8,128)(2,1)} %multiply_convert_fusion.x_ref, bf16[4,192,128]{2,1,0:T(8,128)(2,1)} %fusion.17.pick_ref, bf16[4,384,192]{2,1,0:T(8,128)(2,1)} %pad_maximum_fusion.gate_ref, f32[128,2880]{1,0:T(8,128)} %get-tuple-element.44.mixed_ref, bf16[2880,2880]{1,0:T(8,128)(2,1)} %bitcast.66, ...), custom_call_target="tpu_custom_call" | custom-call | tf_op jit(solution)/shard_map/mixture/pallas_call | solution.py:567
  337.3 2.3 copy.38
  (55 shorter events, 4.7 us)
Async XLA Ops:
  6.5 4.8 %copy-start.4 = (f32[128,4]{0,1:T(4,128)S(1)}, f32[128,4]{0,1:T(4,128)}, u32[]{:S(2)}) copy-start(f32[128,4]{0,1:T(4,128)} %param.21) | copy-start | bytes 6148
  6.5 4.8 %copy-start.2 = (bf16[360,128]{1,0:T(8,128)(2,1)S(1)}, bf16[360,128]{1,0:T(8,128)(2,1)}, u32[]{:S(2)}) copy-start(bf16[360,128]{1,0:T(8,128)(2,1)} %refs_4_.1) | copy-start | bytes 276484
  6.5 4.8 %copy-start.3 = (bf16[360,128]{1,0:T(8,128)(2,1)S(1)}, bf16[360,128]{1,0:T(8,128)(2,1)}, u32[]{:S(2)}) copy-start(bf16[360,128]{1,0:T(8,128)(2,1)} %refs_5_.1) | copy-start | bytes 276484
  6.5 110.3 %all-gather.2.cloned.1.call-start = ((), (), s32[]{:S(2)}) async-start(), calls=%async_computation.1 | async-start | bytes 6635520 | tf_op jit(solution)/shard_map/all_gather | solution.py:655
  8.0 3.3 copy-start.7
  11.3 1.1 copy-start
  70.1 0.9 copy-start.1
  71.0 2.5 copy-start.5
  73.5 0.9 copy-start.6
  74.4 108.5 %reduce-scatter.2.cloned.1.call-start = ((), (), s32[]{:S(2)}) async-start(), calls=%async_computation.2 | async-start | bytes 3768320 | tf_op jit(solution)/shard_map/reduce_scatter | solution.py:701
  76.6 13.9 %collective-permute-start = (bf16[128,128]{1,0:T(8,128)(2,1)S(1)}, bf16[128,128]{1,0:T(8,128)(2,1)S(1)}, u32[]{:S(2)}, u32[]{:S(2)}) collective-permute-start(bf16[128,128]{1,0:T(8,128)(2,1)S(1)} %slice.64), channel_id=1, source_target_pairs={{0,4},{4,8},{8,12},{12,16},{16,20},{20,24},{24,28},{1,5},{5,9},{9,... | collective-permute-start | bytes 98312 | tf_op jit(solution)/shard_map/ppermute | solution.py:20
  80.5 10.1 %collective-permute-start.1 = (bf16[128,128]{0,1:T(8,128)(2,1)S(1)}, bf16[128,128]{0,1:T(8,128)(2,1)S(1)}, u32[]{:S(2)}, u32[]{:S(2)}) collective-permute-start(bf16[128,128]{0,1:T(8,128)(2,1)S(1)} %bitcast.74), channel_id=1, source_target_pairs={{0,4},{4,8},{8,12},{12,16},{16,20},{20,24},{24,28},{1,5},{5,9},{9,... | collective-permute-start | bytes 98312 | tf_op jit(solution)/shard_map/ppermute | solution.py:20
  89.6 0.8 copy-start.11
  124.5 58.4 %copy-start.8 = (bf16[128,2880]{1,0:T(8,128)(2,1)S(1)}, bf16[128,2880]{1,0:T(8,128)(2,1)}, u32[]{:S(2)}) copy-start(bf16[128,2880]{1,0:T(8,128)(2,1)} %copy-done.7) | copy-start | bytes 2211844
  124.6 60.9 %copy-start.10 = (f32[2880]{0:T(1024)S(1)}, f32[2880]{0:T(1024)}, u32[]{:S(2)}) copy-start(f32[2880]{0:T(1024)} %param.19) | copy-start | bytes 34564
  182.9 2.6 copy-start.9
Sparse Core Ops, SparseCore 0:
  74.6 42.2 all-gather.1
  124.7 58.2 reduce-scatter.1

commit v3 on v2

--- a/solution.py
+++ b/solution.py
@@ -69,7 +69,9 @@
 def gather_kernel(n_seq, n_ep, n_line, n_plane, *refs):
     total = n_line + n_plane
     ins, outs, bufs = refs[:total], refs[total : 2 * total], refs[2 * total : 3 * total]
-    own_sem, line_send, line_recv, plane_send, plane_recv, fwd_send = refs[3 * total :]
+    own_sem, line_send, line_recv, plane_send, plane_recv, fwd_send, turn_send, turn_recv = refs[
+        3 * total :
+    ]
     seq, ep = lax.axis_index("seq"), lax.axis_index("ep")
     chips = n_seq // 2
     chip, core = seq // 2, seq % 2
@@ -136,41 +138,69 @@
                         (seq, ep),
                     ).wait_recv()
 
+    square = chips == 4
+    half = ins[n_line].shape[0] // 32 * 16
+    if square:
+        beside, above = chip + 1 - 2 * (chip % 2), lax.rem(chip + 2, 4)
+        across = 3 - chip
+        targets = {0: partner, 1: beside * 2 + core, 2: above * 2 + core}
+    else:
+        targets = {d: lax.rem(chip + d, chips) * 2 + core for d in range(1, chips)}
+        targets[0] = partner
+    peers = [d for d in targets if d != 0]
+
     def plane_copy(i, d):
-        peer = lax.rem(chip + d, chips) * 2 + core
-        if d == 0:
-            peer = partner
         return remote(
             ins[n_line + i],
             outs[n_line + i].at[seq],
             plane_send.at[i, d],
             plane_recv.at[i, seq],
-            (peer, ep),
-        )
-
-    def fwd_copy(i, d):
-        src = lax.rem(chip + d, chips) * 2 + core
+            (targets[d], ep),
+        )
+
+    def fwd_copy(i, d, src):
+        whole = outs[n_line + i].at[src]
+        return remote(whole, whole, fwd_send.at[i, d], plane_recv.at[i, src], (partner, ep))
+
+    def turn_copy(i, d):
+        src = targets[d]
+        rows = ins[n_line + i].shape[0]
+        part = pl.ds(0, half) if d == 1 else pl.ds(half, rows - half)
+        piece = outs[n_line + i].at[src, part]
+        arrival = plane_recv if d == 1 else turn_recv
         return remote(
-            outs[n_line + i].at[src],
-            outs[n_line + i].at[src],
-            fwd_send.at[i, d],
-            plane_recv.at[i, src],
-            (partner, ep),
+            piece, piece, turn_send.at[i, d], arrival.at[i, src], (targets[3 - d], ep)
         )
 
     def plane_arrived(i, src):
-        remote(
-            ins[n_line + i],
-            outs[n_line + i].at[src],
-            plane_send.at[i, 0],
-            plane_recv.at[i, src],
-            (partner, ep),
-        ).wait_recv()
+        whole = outs[n_line + i].at[src]
+        remote(whole, whole, plane_send.at[i, 0], plane_recv.at[i, src], (partner, ep)).wait_recv()
+
+    def halves_arrived(i, src):
+        rows = ins[n_line + i].shape[0]
+        for part, arrival in ((pl.ds(0, half), plane_recv), (pl.ds(half, rows - half), turn_recv)):
+            piece = outs[n_line + i].at[src, part]
+            remote(piece, piece, plane_send.at[i, 0], arrival.at[i, src], (partner, ep)).wait_recv()
+
+    def near_arrived(which):
+        for i in which:
+            for d in peers:
+                plane_arrived(i, targets[d])
+                if square:
+                    turn_copy(i, d).start()
+                fwd_copy(i, d, targets[d]).start()
+
+    def across_arrived(which):
+        if square:
+            for i in which:
+                halves_arrived(i, across * 2 + core)
+                fwd_copy(i, 3, across * 2 + core).start()
 
     every = range(n_line)
+    last = n_plane - 1
     line_copies(0, every, lambda c: c.start())
     for i in range(n_plane):
-        for d in range(chips):
+        for d in (*peers, 0):
             plane_copy(i, d).start()
     for i in range(total):
         pltpu.make_async_copy(ins[i], bufs[i], own_sem.at[i]).start()
@@ -181,24 +211,28 @@
     for step in range(1, n_ep - 1):
         line_arrived(step, every)
         line_copies(step, every, lambda c: c.start())
-    for i in range(n_plane):
-        for d in range(1, chips):
-            plane_arrived(i, lax.rem(chip + d, chips) * 2 + core)
-            fwd_copy(i, d).start()
+        if step == 1:
+            near_arrived(range(last))
+    near_arrived([last])
+    across_arrived(range(n_plane))
     line_arrived(n_ep - 1, every)
     for i in range(n_plane):
-        for d in range(chips):
-            plane_arrived(i, lax.rem(chip + d, chips) * 2 + 1 - core)
+        for other in range(chips):
+            plane_arrived(i, other * 2 + 1 - core)
     for i in range(total):
         mine = outs[i].at[ep if i < n_line else seq]
         pltpu.make_async_copy(bufs[i], mine, own_sem.at[i]).wait()
     for step in range(n_ep - 1):
         line_copies(step, every, lambda c: c.wait_send())
     for i in range(n_plane):
-        for d in range(chips):
+        for d in (*peers, 0):
             plane_copy(i, d).wait_send()
-        for d in range(1, chips):
-            fwd_copy(i, d).wait_send()
+        for d in peers:
+            fwd_copy(i, d, targets[d]).wait_send()
+            if square:
+                turn_copy(i, d).wait_send()
+        if square:
+            fwd_copy(i, 3, across * 2 + core).wait_send()
 
 
 def gathered(line, plane):
@@ -221,6 +255,8 @@
             sem((n_plane, chips)),
             sem((n_plane, n_seq)),
             sem((n_plane, chips)),
+            sem((n_plane, 3)),
+            sem((n_plane, n_seq)),
         ],
         compiler_params=pltpu.CompilerParams(
             collective_id=0, has_side_effects=True, vmem_limit_bytes=16 << 20
@@ -649,12 +685,10 @@
     capacity = -(-capacity // 8) * 8
     (normed_all, line_slots, line_gates, *shard_rows) = gathered(
         (normed_own, slot_of(expert_ids, capacity).T, expert_gates.T),
-        (query_weight, key_weight, value_weight),
-    )
-    normed_all, out_cols = lax.optimization_barrier((normed_all, output_weight.T))
-    out_rows = lax.all_gather(out_cols, "seq", axis=0, tiled=True)
+        (query_weight, key_weight, value_weight, output_weight.T),
+    )
     normed_all = normed_all.reshape(tok_rows, width_dim)
-    shard_rows = [rows.reshape(width_dim, -1) for rows in shard_rows]
+    *shard_rows, out_rows = [rows.reshape(width_dim, -1) for rows in shard_rows]
     q_lin, k_lin, v_lin = tuple(
         (
             jnp.dot(normed_all, weight_rows, preferred_element_type=jnp.float32)

time: 351 us -> 349 us (level)
  waiting for transfers between devices: 68.1 us -> 55.1 us
  local copies, waits for them, and re-layouts: 10.6 us -> 15.2 us
  Pallas kernels: 208 us -> 212 us
    all_gather x1 -> x0, waiting for transfers between devices: 12.5 us -> none  [body(): out_rows = lax.all_gather(out_cols, 'seq', axis=0, tiled=True)]
    pallas_call x1, Pallas kernels: 57.6 us -> 61.8 us  [gathered(): pl.pallas_call(functools.partial(gather_kernel, n_seq, n_ep, n_line, n_pl...]
    unnamed x26 -> x36, local copies, waits for them, and re-layouts: 7.77 us -> 11.2 us
  transfers between devices with their start and end apart: 4 -> 3, of which waited for: 2 -> 1; matrix products, arithmetic and copies ran while one was open for 8% -> 4% of each run, Pallas kernels for 0% -> 0%
where the time goes in v3:
time: 349 us; the launch traced here: 345 us
  Pallas kernels  212 us (61%)
  waiting for transfers between devices  55.1 us (16%)
  matrix products  26.4 us (8%)
  other arithmetic  15.7 us (4%)
  local copies, waits for them, and re-layouts  15.2 us (4%)
  between operations  14.1 us (4%)
  starting transfers between devices  6.09 us (2%)
    pallas_call x1, Pallas kernels, mixture(): pl.pallas_call(functools.partial(moe_kernel, n_seq, n_ep, cap), out_shape...  150 us
    pallas_call x1, Pallas kernels, gathered(): pl.pallas_call(functools.partial(gather_kernel, n_seq, n_ep, n_line, n_pl...  61.8 us
    reduce_scatter x1, waiting for transfers between devices, body(): lax.psum_scatter(by_rows(head_partial), 'ep', scatter_dimension=0, tiled=...  55 us
    unnamed x36, local copies, waits for them, and re-layouts  11.2 us
    another operation x2, matrix products, by_rows(): return with_layout_constraint(x, Layout(tuple(range(x.ndim))))  7.79 us
    dot_general x1, matrix products, attend(): jnp.einsum('kgqj,jkd->qkgd', weights, val_rows, preferred_element_type=jn...  7.64 us
  transfers between devices with their start and end apart: 3, of which 1 were waited for; matrix products, arithmetic and copies ran while one was open for 4% of the time, Pallas kernels for 0%

profile of v3, /device:TPU:0, one launch (start us, length us, event | category | flops | bytes accessed | tf_op | source)
XLA Modules:
  0.0 344.9 jit_solution(17848729385886851819)
XLA Ops:
  6.5 1.5 copy.31
  10.3 0.9 fusion.5.refs_0_
  11.4 1.1 copy-done
  12.5 1.1 copy-done.1
  13.6 61.8 %gather.1 = (bf16[4,128,2880]{2,1,0:T(8,128)(2,1)S(1)}, s32[4,4,128]{2,1,0:T(4,128)S(1)}, f32[4,4,128]{2,1,0:T(4,128)S(1)}, bf16[8,360,1024]{2,1,0:T(8,128)(2,1)...) custom-call(bf16[128,2880]{1,0:T(8,128)(2,1)S(1)} %fusion.5.refs_0_, ...), custom_call_target="tpu_custom_call" | custom-call | tf_op jit(solution)/shard_map/gather/pallas_call | solution.py:245
  75.4 0.9 copy-done.2
  76.3 2.5 copy-done.6
  78.8 2.6 copy-done.7
  81.4 0.9 convolution_convert_fusion.1
  83.6 2.9 collective-permute-start
  86.5 2.2 fusion.34
  89.8 3.1 collective-permute-start.1
  92.9 5.5 %fusion.35 = f32[512,1024]{0,1:T(8,128)S(1)} fusion(bf16[512,2880]{1,0:T(8,128)(2,1)S(1)} %bitcast.62, bf16[2880,1024]{1,0:T(8,128)(2,1)} %bitcast.69), kind=kOutput, calls=%fused_computation.82 | convolution fusion | flops 3019898880 | bytes 10944512 | tf_op jit(solution)/shard_map/layout_constraint | solution.py:656
  101.0 3.9 %fusion.1 = (f32[2,8,512]{2,1,0:T(8,128)S(1)}, f32[2,640,512,8]{2,1,3,0:T(8,128)S(1)}) fusion(pred[512,640]{0,1:T(8,128)(4,1)S(1)} %fusion.8, bf16[512,2,8,32]{0,3,2,1:T(8,128)(2,1)S(1)} %bitcast.76, bf16[512,2,8,32]{0,3,2,1:T(8,128)(2,1)S(1)} %bitcast.75, bf16[512,2,32]{0,2,1:T(8,128)(2,1)S(1)} %get-tuple-element.45, ...), kind=kOutput, calls=%fused_computation.4 | convolution fusion | flops 689397760 | bytes 22544384 | tf_op jit(solution)/shard_map/while/body/eval_jaxpr/qkgd,jkd->kgqj/dot_general | solution.py:43
  105.0 4.5 %fusion = f32[2,8,512]{2,1,0:T(8,128)S(1)} fusion(f32[2,640,512,8]{2,1,3,0:T(8,128)S(1)} %get-tuple-element.60, f32[2,8,512]{2,1,0:T(8,128)S(1)} %broadcast_maximum_fusion, pred[512,640]{0,1:T(8,128)(4,1)S(1)} %fusion.8), kind=kLoop, calls=%fused_computation.3 | loop fusion | flops 20963328 | bytes 21364736 | tf_op jit(solution)/shard_map/while/body/eval_jaxpr/reduce_sum | solution.py:52
  109.7 7.6 %fusion.6 = bf16[2,64,8,512]{3,1,2,0:T(8,128)(2,1)} fusion(bf16[640,2,64,1]{0,2,3,1:T(8,128)(2,1)} %bitcast.77, f32[2,640,512,8]{2,1,3,0:T(8,128)S(1)} %get-tuple-element.60, f32[2,8,512]{2,1,0:T(8,128)S(1)} %exponential_add_fusion, f32[2,8,512]{2,1,0:T(8,128)S(1)} %broadcast_maximum_fusion, pred[512,640]{0,1:T(8,128)(4,1)S(1)} %fusion.8), kind=kOutput, calls=%fused_computation.17 | convolution fusion | flops 697827328 | bytes 22577152 | tf_op jit(solution)/shard_map/while/body/eval_jaxpr/kgqj,jkd->qkgd/dot_general | solution.py:54
  117.3 6.1 %convolution_convert_fusion = bf16[512,2880]{1,0:T(8,128)(2,1)} fusion(bf16[512,1024]{0,1:T(8,128)(2,1)} %bitcast.90, bf16[2880,1024]{1,0:T(8,128)(2,1)S(1)} %bitcast.68), kind=kOutput, calls=%fused_computation.6 | convolution fusion | flops 3021373440 | bytes 9895936 | tf_op jit(solution)/shard_map/dot_general | solution.py:732
  124.3 1.0 pad_maximum_fusion.gate_ref
  125.3 0.9 fusion.17.pick_ref
  126.2 55.0 %reduce-scatter.2.cloned.1.call-done = bf16[128,2880]{1,0:T(8,128)(2,1)} async-done(((bf16[512,2880]{1,0:T(8,128)(2,1)}), bf16[128,2880]{1,0:T(8,128)(2,1)}) %reduce-scatter.2.cloned.1.call-update) | async-done | bytes 737296 | tf_op jit(solution)/shard_map/reduce_scatter | solution.py:735
  181.2 2.6 convert_add_fusion
  183.8 1.1 multiply_convert_fusion.x_ref
  184.9 150.4 %mixture.1 = bf16[128,2880]{1,0:T(8,128)(2,1)} custom-call(bf16[128,2880]{1,0:T(8,128)(2,1)} %multiply_convert_fusion.x_ref, bf16[4,192,128]{2,1,0:T(8,128)(2,1)} %fusion.17.pick_ref, bf16[4,384,192]{2,1,0:T(8,128)(2,1)} %pad_maximum_fusion.gate_ref, f32[128,2880]{1,0:T(8,128)} %get-tuple-element.42.mixed_ref, bf16[2880,2880]{1,0:T(8,128)(2,1)} %bitcast.71, ...), custom_call_target="tpu_custom_call" | custom-call | tf_op jit(solution)/shard_map/mixture/pallas_call | solution.py:603
  335.3 2.3 copy.38
  (63 shorter events, 8.0 us)
Async XLA Ops:
  6.5 4.8 %copy-start.5 = (f32[128,4]{0,1:T(4,128)S(1)}, f32[128,4]{0,1:T(4,128)}, u32[]{:S(2)}) copy-start(f32[128,4]{0,1:T(4,128)} %param.21) | copy-start | bytes 6148
  6.5 4.8 %copy-start.3 = (bf16[360,128]{1,0:T(8,128)(2,1)S(1)}, bf16[360,128]{1,0:T(8,128)(2,1)}, u32[]{:S(2)}) copy-start(bf16[360,128]{1,0:T(8,128)(2,1)} %refs_4_.1) | copy-start | bytes 276484
  6.5 4.8 %copy-start.4 = (bf16[360,128]{1,0:T(8,128)(2,1)S(1)}, bf16[360,128]{1,0:T(8,128)(2,1)}, u32[]{:S(2)}) copy-start(bf16[360,128]{1,0:T(8,128)(2,1)} %refs_5_.1) | copy-start | bytes 276484
  6.5 174.7 %reduce-scatter.2.cloned.1.call-start = ((), (), s32[]{:S(2)}) async-start(), calls=%async_computation.1 | async-start | bytes 3768320 | tf_op jit(solution)/shard_map/reduce_scatter | solution.py:735
  8.0 3.3 copy-start.8
  11.3 1.1 copy-start
  12.5 1.1 copy-start.1
  75.4 0.9 copy-start.2
  76.3 2.5 copy-start.6
  78.8 2.6 copy-start.7
  82.3 0.6 copy-start.11
  83.6 15.8 %collective-permute-start = (bf16[128,128]{1,0:T(8,128)(2,1)}, bf16[128,128]{1,0:T(8,128)(2,1)}, u32[]{:S(2)}, u32[]{:S(2)}) collective-permute-start(bf16[128,128]{1,0:T(8,128)(2,1)} %slice.64), channel_id=1, source_target_pairs={{0,4},{4,8},{8,12},{12,16},{16,20},{20,24},{24,28},{1,5},{5,9},{9,... | collective-permute-start | bytes 98312 | tf_op jit(solution)/shard_map/ppermute | solution.py:20
  89.8 11.3 %collective-permute-start.1 = (bf16[128,128]{0,1:T(8,128)(2,1)}, bf16[128,128]{0,1:T(8,128)(2,1)}, u32[]{:S(2)}, u32[]{:S(2)}) collective-permute-start(bf16[128,128]{0,1:T(8,128)(2,1)} %bitcast.10), channel_id=1, source_target_pairs={{0,4},{4,8},{8,12},{12,16},{16,20},{20,24},{24,28},{1,5},{5,9},{9,... | collective-permute-start | bytes 98312 | tf_op jit(solution)/shard_map/ppermute | solution.py:20
  98.5 0.8 copy-start.14
  98.5 0.9 copy-start.12
  105.0 12.3 %slice-start = ((s8[5898240]{0:T(1024)(128)(4,1)}), s8[4194304]{0:T(1024)(128)(4,1)S(1)}, s32[]{:S(2)}) async-start(s8[5898240]{0:T(1024)(128)(4,1)} %bitcast.66), calls=%async_computation.2 | async-start | bytes 8388608
  109.7 7.7 %slice-start.1 = ((s8[5898240]{0:T(1024)(128)(4,1)}), s8[1703936]{0:T(1024)(128)(4,1)S(1)}, s32[]{:S(2)}) async-start(s8[5898240]{0:T(1024)(128)(4,1)} %bitcast.66), calls=%async_computation.3 | async-start | bytes 3407872
  123.4 57.8 %copy-start.9 = (bf16[128,2880]{1,0:T(8,128)(2,1)S(1)}, bf16[128,2880]{1,0:T(8,128)(2,1)}, u32[]{:S(2)}) copy-start(bf16[128,2880]{1,0:T(8,128)(2,1)} %copy-done.8) | copy-start | bytes 2211844
  123.5 60.3 %copy-start.13 = (f32[2880]{0:T(1024)S(1)}, f32[2880]{0:T(1024)}, u32[]{:S(2)}) copy-start(f32[2880]{0:T(1024)} %param.19) | copy-start | bytes 34564
  181.2 2.6 copy-start.10
Sparse Core Ops, SparseCore 0:
  123.6 57.5 reduce-scatter.1

commit v4 on v3

--- a/solution.py
+++ b/solution.py
@@ -286,18 +286,26 @@
     return [(c, min(most, width - c)) for c in range(0, width, most)]
 
 
-def moe_kernel(
+def pieces(width):
+    return [(c, min(1024, width - c), min(1024, -(-width // 128) * 128 - c)) for c in range(0, width, 1024)]
+
+
+def layer_kernel(
     n_seq,
     n_ep,
     cap,
-    x_ref,
+    att_ref,
+    wo_hbm,
+    rows_ref,
+    gain_ref,
     pick_ref,
     gate_ref,
-    mixed_ref,
     win_hbm,
     wout_hbm,
     out_ref,
+    x_ref,
     held,
+    parts,
     staged,
     arrived,
     back,
@@ -309,6 +317,9 @@
     w_in,
     w_out,
     weight_sem,
+    wo_sem,
+    head_send,
+    head_recv,
     line_send,
     line_recv,
     send,
@@ -321,13 +332,27 @@
     sum_recv,
 ):
     seq, ep = lax.axis_index("seq"), lax.axis_index("ep")
-    rows, width = mixed_ref.shape
+    rows, width = rows_ref.shape
     slots = n_seq * cap
     hidden = wout_hbm.shape[0]
+    depth = att_ref.shape[1]
+    cols = pieces(width)
+    n_cols = len(cols)
+    scale_at = x_ref.shape[1] - 128
+    padded = back.shape[3]
     in_copy = pltpu.make_async_copy(win_hbm, w_in, weight_sem.at[0])
     out_copy = pltpu.make_async_copy(wout_hbm, w_out, weight_sem.at[1])
+
+    def wo_place(i):
+        return w_out.at[0 : cols[i][1], (i % 2) * depth : (i % 2 + 1) * depth]
+
+    def wo_copy(i):
+        c, size, _ = cols[i]
+        return pltpu.make_async_copy(wo_hbm.at[pl.ds(c, size)], wo_place(i), wo_sem.at[i])
+
+    for i in range(min(2, n_cols)):
+        wo_copy(i).start()
     in_copy.start()
-    out_copy.start()
     signal_all(pltpu.get_barrier_semaphore(), n_seq, n_ep, seq, ep, (-1, 1))
 
     def spread(buffer, c, size, value):
@@ -338,38 +363,42 @@
         slabs = [buffer[first + s, :, c : c + size].astype(jnp.float32) for s in range(count)]
         return jnp.concatenate(slabs, axis=0).astype(jnp.bfloat16)
 
-    def relay(step, src, away, act_on):
+    def relay(step, src, away, i, act_on):
+        piece = pl.ds(i * 1024, 1024)
+
         @pl.when((src >= 0) & (src < n_ep) & (ep + away >= 0) & (ep + away < n_ep))
         def _():
             act_on(
                 remote(
-                    x_ref if step == 0 else held.at[src],
-                    held.at[src],
-                    line_send.at[(away + 1) // 2, step],
-                    line_recv.at[src],
+                    x_ref.at[:, piece] if step == 0 else held.at[src, :, piece],
+                    held.at[src, :, piece],
+                    line_send.at[(away + 1) // 2, step, i],
+                    line_recv.at[src, i],
                     (seq, ep + away),
                 )
             )
 
-    def part(src, d):
+    def part(src, d, i):
         peer = lax.rem(seq + d, n_seq)
+        piece = pl.ds(i * 1024, 1024)
         return remote(
-            staged.at[src, peer],
-            arrived.at[src, seq],
-            send.at[src, d],
-            recv.at[src, seq],
+            staged.at[src, peer, :, piece],
+            arrived.at[src, seq, :, piece],
+            send.at[src, d, i],
+            recv.at[src, seq, i],
             (peer, ep),
         )
 
-    def own_part(src):
+    def own_part(src, i):
+        piece = pl.ds(i * 1024, 1024)
         return pltpu.make_async_copy(
-            staged.at[src, seq], arrived.at[src, seq], own.at[src]
+            staged.at[src, seq, :, piece], arrived.at[src, seq, :, piece], own.at[src, i]
         )
 
     def back_part(src, d):
         peer = lax.rem(seq + d, n_seq)
         return remote(
-            staged.at[src, peer],
+            staged.at[src, peer, :, pl.ds(0, padded)],
             back.at[src, seq],
             back_send.at[src, d],
             back_recv.at[src, seq],
@@ -378,27 +407,33 @@
 
     def back_own_part(src):
         return pltpu.make_async_copy(
-            staged.at[src, seq], back.at[src, seq], back_own.at[src]
+            staged.at[src, seq, :, pl.ds(0, padded)], back.at[src, seq], back_own.at[src]
         )
 
     def landing(at, step, way):
         return jnp.where(way == -1, n_ep, at) if step == 1 else at
 
-    def sum_copy(at, step, way, i):
-        c, size = column_chunks(width)[i]
+    def line_sum(buffer, at, step, way, i, send_sem, recv_sem):
+        c, _, size = cols[i]
         slot = landing(at, step, way)
         return remote(
-            held.at[at, :, c : c + size],
-            sums.at[slot, :, c : c + size],
-            sum_send.at[at, i],
-            sum_recv.at[slot, i],
+            buffer.at[at, :, pl.ds(c, size)],
+            sums.at[slot, :, pl.ds(c, size)],
+            send_sem.at[at, i],
+            recv_sem.at[slot, i],
             (seq, ep + way),
         )
 
-    def sum_arrived(slot, i):
-        c, size = column_chunks(width)[i]
-        piece = sums.at[slot, :, c : c + size]
-        remote(piece, piece, sum_send.at[0, 0], sum_recv.at[slot, i], (seq, ep)).wait_recv()
+    def head_copy(at, step, way, i):
+        return line_sum(parts, at, step, way, i, head_send, head_recv)
+
+    def sum_copy(at, step, way, i):
+        return line_sum(held, at, step, way, i, sum_send, sum_recv)
+
+    def sum_arrived(recv_sem, slot, i):
+        c, _, size = cols[i]
+        piece = sums.at[slot, :, pl.ds(c, size)]
+        remote(piece, piece, sum_send.at[0, 0], recv_sem.at[slot, i], (seq, ep)).wait_recv()
 
     def each(d, act_on):
         at = ep + d
@@ -407,35 +442,35 @@
         def _():
             act_on(at)
 
-    def hand_out(src, rows_ref):
-        for c, size in column_chunks(width):
-            picked = jnp.dot(
-                pick_ref[src], rows_ref[:, c : c + size], preferred_element_type=jnp.float32
-            )
-            spread(staged.at[src], c, size, picked)
+    def hand_out(src, from_ref, i):
+        c = i * 1024
+        picked = jnp.dot(
+            pick_ref[src], from_ref[:, c : c + 1024], preferred_element_type=jnp.float32
+        )
+        spread(staged.at[src], c, 1024, picked)
         for d in range(1, n_seq):
-            part(src, d).start()
-        own_part(src).start()
+            part(src, d, i).start()
+        own_part(src, i).start()
 
     def expert(src):
-        own_part(src).wait()
-        for d in range(1, n_seq):
-            peer = lax.rem(seq + d, n_seq)
-            remote(
-                staged.at[src, seq],
-                arrived.at[src, peer],
-                send.at[src, 0],
-                recv.at[src, peer],
-                (peer, ep),
-            ).wait_recv()
+        for i in range(n_cols):
+            own_part(src, i).wait()
+            for d in range(1, n_seq):
+                peer = lax.rem(seq + d, n_seq)
+                piece = arrived.at[src, peer, :, pl.ds(i * 1024, 1024)]
+                remote(
+                    piece, piece, send.at[src, 0, i], recv.at[src, peer, i], (peer, ep)
+                ).wait_recv()
 
         group = n_seq if slots % 16 else 2
         for s in range(0, n_seq, group):
-            taken[s * cap : (s + group) * cap, :] = together(arrived.at[src], 0, width, s, group)
+            taken[s * cap : (s + group) * cap, :] = together(
+                arrived.at[src], 0, taken.shape[1], s, group
+            )
 
         def up_columns(c, size):
             joined[:, pl.ds(c, size)] = jnp.dot(
-                taken[...], w_in[:, pl.ds(c, size)], preferred_element_type=jnp.float32
+                taken[:, 0:width], w_in[:, pl.ds(c, size)], preferred_element_type=jnp.float32
             )
 
         @pl.loop(0, width // 512)
@@ -448,12 +483,15 @@
         @pl.loop(0, slots // 16)
         def _(i):
             r = pl.ds(pl.multiple_of(i * 16, 16), 16)
-            gate = joined[r, 0:hidden]
-            up = joined[r, hidden : 2 * hidden]
+            scales = taken[r, scale_at : scale_at + 128].astype(jnp.float32)
+            scale = jnp.sum(scales, axis=1, keepdims=True)
+            gate = joined[r, 0:hidden] * scale
+            up = joined[r, hidden : 2 * hidden] * scale
             act[r, :] = ((up + 1.0) * gate * jax.nn.sigmoid(1.702 * gate)).astype(jnp.bfloat16)
 
-        for d in range(1, n_seq):
-            part(src, d).wait_send()
+        for i in range(n_cols):
+            for d in range(1, n_seq):
+                part(src, d, i).wait_send()
 
         def down_columns(c, size):
             value = jnp.dot(
@@ -475,24 +513,26 @@
         back_own_part(at).wait()
         for d in range(1, n_seq):
             peer = lax.rem(seq + d, n_seq)
+            piece = back.at[at, peer]
             remote(
-                staged.at[at, seq],
-                back.at[at, peer],
-                back_send.at[at, 0],
-                back_recv.at[at, peer],
-                (peer, ep),
+                piece, piece, back_send.at[at, 0], back_recv.at[at, peer], (peer, ep)
             ).wait_recv()
-        for i, (c, size) in enumerate(column_chunks(width)):
+        for i, (c, size, _) in enumerate(cols):
             results = together(back.at[at], c, size, 0, n_seq)
             three = jnp.dot(gate_ref[at], results, preferred_element_type=jnp.float32)
             finish(i, c, size, three[:rows] + three[rows : 2 * rows] + three[2 * rows :])
 
-    def pass_on(step, way):
+    def in_line(step, way, act_on):
         at = ep + way * step
 
         @pl.when((at >= 0) & (at < n_ep))
         def _():
-            relay(step, at, -way, lambda c: c.wait_send())
+            act_on(at)
+
+    def pass_on(step, way):
+        def one(at):
+            for i in range(n_cols):
+                relay(step, at, -way, i, lambda c: c.wait_send())
 
             def finish(i, c, size, value):
                 before = ep - way
@@ -500,7 +540,7 @@
 
                 @pl.when(joins)
                 def _():
-                    sum_arrived(at, i)
+                    sum_arrived(sum_recv, at, i)
                     sofar = sums[at, :, c : c + size].astype(jnp.float32)
                     held[at, :, c : c + size] = (value + sofar).astype(jnp.bfloat16)
 
@@ -512,31 +552,137 @@
 
             gather_up(at, finish)
 
-    relay(0, ep, 1, lambda c: c.start())
-    relay(0, ep, -1, lambda c: c.start())
-    hand_out(ep, x_ref)
-    for step in range(1, n_ep):
+        in_line(step, way, one)
+
+    toward = jnp.where(2 * ep < n_ep, 1, -1)
+    at_end = (ep == 0) | (ep == n_ep - 1)
+
+    def project(i):
+        c, size, _ = cols[i]
+        wo_copy(i).wait()
+        place = wo_place(i)
+
+        def columns(first, count):
+            value = lax.dot_general(
+                att_ref[...],
+                place[pl.ds(first, count), :],
+                (((1,), (1,)), ((), ())),
+                preferred_element_type=jnp.float32,
+            ).astype(jnp.bfloat16)
+            for at in range(n_ep):
+                parts[at, :, pl.ds(c + first, count)] = value[at * rows : (at + 1) * rows]
+
+        @pl.loop(0, size // 256)
+        def _(j):
+            columns(pl.multiple_of(j * 256, 256), 256)
+
+        if size % 256:
+            columns(size // 256 * 256, size % 256)
+        if i + 2 < n_cols:
+            wo_copy(i + 2).start()
+
+    def head_on(step, way, i):
+        c, size, _ = cols[i]
+
+        def one(at):
+            before = ep - way
+
+            @pl.when((before >= 0) & (before < n_ep))
+            def _():
+                sum_arrived(head_recv, at, i)
+                mixed = parts[at, :, c : c + size].astype(jnp.float32) + sums[
+                    at, :, c : c + size
+                ].astype(jnp.float32)
+                parts[at, :, c : c + size] = mixed.astype(jnp.bfloat16)
+
+            head_copy(at, step, way, i).start()
+
+        in_line(step, way, one)
+
+    def send_heads(i):
+        for step in range(n_ep - 1, 0, -1):
+            head_on(step, toward, i)
+        for step in range(n_ep // 2 - 1, 0, -1):
+            head_on(step, -toward, i)
+
+    squares = []
+
+    def own_rows(i):
+        c, size, _ = cols[i]
+        part_own = parts[ep, :, c : c + size].astype(jnp.float32)
+        mine[:, c : c + size] = rows_ref[:, c : c + size].astype(jnp.float32) + part_own
+
+        def add_from(slot):
+            sum_arrived(head_recv, slot, i)
+            mine[:, c : c + size] += sums[slot, :, c : c + size].astype(jnp.float32)
+
+        @pl.when(ep > 0)
+        def _():
+            add_from(ep)
+
+        @pl.when(ep < n_ep - 1)
+        def _():
+            add_from(n_ep)
+
+        value = mine[:, c : c + size]
+        squares.append(jnp.sum(value * value, axis=1, keepdims=True))
+        x_ref[:, c : c + size] = (value * gain_ref[:, c : c + size]).astype(jnp.bfloat16)
+        if i == n_cols - 1:
+            scale = lax.rsqrt(sum(squares) / width + 1e-05)
+            high = scale.astype(jnp.bfloat16).astype(jnp.float32)
+            middle = (scale - high).astype(jnp.bfloat16).astype(jnp.float32)
+            low = scale - high - middle
+            lane = lax.broadcasted_iota(jnp.int32, (rows, 128), 1)
+            tile = jnp.where(lane == 0, high, jnp.where(lane == 1, middle, 0.0))
+            tile = jnp.where(lane == 2, low, tile)
+            x_ref[:, scale_at : scale_at + 128] = tile.astype(jnp.bfloat16)
+            gap = scale_at - width
+            if gap:
+                x_ref[:, width:scale_at] = jnp.zeros((rows, gap), jnp.bfloat16)
+        for way in (1, -1):
+            relay(0, ep, way, i, lambda c: c.start())
+        hand_out(ep, x_ref, i)
+
+    def from_line(step, i):
         for way in (1, -1):
             src = ep - way * step
 
             @pl.when((src >= 0) & (src < n_ep))
             def _():
+                piece = held.at[src, :, pl.ds(i * 1024, 1024)]
                 remote(
-                    x_ref, held.at[src], line_send.at[0, 0], line_recv.at[src], (seq, ep)
+                    piece, piece, line_send.at[0, 0, 0], line_recv.at[src, i], (seq, ep)
                 ).wait_recv()
 
-            relay(step, src, way, lambda c: c.start())
+            relay(step, src, way, i, lambda c: c.start())
         for way in (1, -1):
-            each(-way * step, lambda at: hand_out(at, held.at[at]))
-        if step == 1:
-            in_copy.wait()
-            out_copy.wait()
-            expert(ep)
+            each(-way * step, lambda at: hand_out(at, held.at[at], i))
+
+    jobs = []
+    for i in range(n_cols):
+        jobs.append((3 * i - 1.5, 0, i))
+        jobs.append((3 * i + 3, 1, i))
+        for step in range(1, n_ep):
+            jobs.append((3 * i + 3 + step, 2 + step, i))
+    for _, kind, i in sorted(jobs):
+        if kind == 0:
+            project(i)
+            send_heads(i)
+            if i == n_cols - 1:
+                out_copy.start()
+        elif kind == 1:
+            own_rows(i)
         else:
-            for way in (1, -1):
-                each(-way * (step - 1), expert)
-    toward = jnp.where(2 * ep < n_ep, 1, -1)
-    at_end = (ep == 0) | (ep == n_ep - 1)
+            from_line(kind - 2, i)
+            if i == n_cols - 1:
+                step = kind - 2
+                if step == 1:
+                    in_copy.wait()
+                    out_copy.wait()
+                    expert(ep)
+                else:
+                    for way in (1, -1):
+                        each(-way * (step - 1), expert)
 
     @pl.when(at_end)
     def _():
@@ -555,7 +701,7 @@
         pass_on(step, toward)
 
     def keep(i, c, size, value):
-        mine[:, c : c + size] = mixed_ref[:, c : c + size] + value
+        mine[:, c : c + size] += value
 
     gather_up(ep, keep)
 
@@ -563,8 +709,8 @@
         pass_on(step, -toward)
 
     def add(slot):
-        for i, (c, size) in enumerate(column_chunks(width)):
-            sum_arrived(slot, i)
+        for i, (c, size, _) in enumerate(cols):
+            sum_arrived(sum_recv, slot, i)
             mine[:, c : c + size] += sums[slot, :, c : c + size].astype(jnp.float32)
 
     @pl.when(ep > 0)
@@ -575,65 +721,76 @@
     def _():
         add(n_ep)
 
-    for c, size in column_chunks(width):
+    for c, size, _ in cols:
         out_ref[:, c : c + size] = mine[:, c : c + size].astype(jnp.bfloat16)
-    for step in range(1, n_ep):
+    for i in range(n_cols):
+        for step in range(1, n_ep):
+            for way in (1, -1):
+
+                def sent(at):
+                    head_copy(at, step, way, i).wait_send()
+                    sum_copy(at, step, way, i).wait_send()
+
+                each(way * step, sent)
         for way in (1, -1):
-
-            def sent(at):
-                for i in range(len(column_chunks(width))):
-                    sum_copy(at, step, way, i).wait_send()
-
-            each(way * step, sent)
-    for way in (1, -1):
-        relay(0, ep, way, lambda c: c.wait_send())
+            relay(0, ep, way, i, lambda c: c.wait_send())
     for src in range(n_ep):
         for d in range(1, n_seq):
             back_part(src, d).wait_send()
 
 
-def mixture(rows_in, picks, gates, mixed, w_in, w_out, cap):
+def mixture(attended, out_rows, own, gain, picks, gates, w_in, w_out, cap):
     n_seq, n_ep = lax.axis_size("seq"), lax.axis_size("ep")
-    rows, width = mixed.shape
+    rows, width = own.shape
     hidden = w_out.shape[0]
     slots = n_seq * cap
+    n_cols = len(pieces(width))
+    padded = -(-width // 128) * 128
+    wide = n_cols * 1024
+    if wide < padded + 128 or w_out.shape[0] < 1024 or width < 2 * attended.shape[1]:
+        raise ValueError("unexpected widths")
     sem = pltpu.SemaphoreType.DMA
     vmem = pl.BlockSpec(memory_space=pltpu.VMEM)
     anywhere = pl.BlockSpec(memory_space=pl.ANY)
     return pl.pallas_call(
-        functools.partial(moe_kernel, n_seq, n_ep, cap),
+        functools.partial(layer_kernel, n_seq, n_ep, cap),
         out_shape=jax.ShapeDtypeStruct((rows, width), jnp.bfloat16),
-        in_specs=[vmem, vmem, vmem, vmem, anywhere, anywhere],
+        in_specs=[vmem, anywhere, vmem, vmem, vmem, vmem, anywhere, anywhere],
         out_specs=vmem,
         scratch_shapes=[
-            pltpu.VMEM((n_ep, rows, width), jnp.bfloat16),
-            pltpu.VMEM((n_ep, n_seq, cap, width), jnp.bfloat16),
-            pltpu.VMEM((n_ep, n_seq, cap, width), jnp.bfloat16),
-            pltpu.VMEM((n_ep, n_seq, cap, width), jnp.bfloat16),
-            pltpu.VMEM((n_ep + 1, rows, width), jnp.bfloat16),
+            pltpu.VMEM((rows, wide), jnp.bfloat16),
+            pltpu.VMEM((n_ep, rows, wide), jnp.bfloat16),
+            pltpu.VMEM((n_ep, rows, padded), jnp.bfloat16),
+            pltpu.VMEM((n_ep, n_seq, cap, wide), jnp.bfloat16),
+            pltpu.VMEM((n_ep, n_seq, cap, wide), jnp.bfloat16),
+            pltpu.VMEM((n_ep, n_seq, cap, padded), jnp.bfloat16),
+            pltpu.VMEM((n_ep + 1, rows, padded), jnp.bfloat16),
             pltpu.VMEM((rows, width), jnp.float32),
-            pltpu.VMEM((slots, width), jnp.bfloat16),
+            pltpu.VMEM((slots, wide), jnp.bfloat16),
             pltpu.VMEM((slots, width), jnp.float32),
             pltpu.VMEM((slots, hidden), jnp.bfloat16),
             pltpu.VMEM(w_in.shape, jnp.bfloat16),
             pltpu.VMEM(w_out.shape, jnp.bfloat16),
             sem((2,)),
-            sem((2, n_ep)),
-            sem((n_ep,)),
+            sem((n_cols,)),
+            sem((n_ep, n_cols)),
+            sem((n_ep + 1, n_cols)),
+            sem((2, n_ep, n_cols)),
+            sem((n_ep, n_cols)),
+            sem((n_ep, n_seq, n_cols)),
+            sem((n_ep, n_seq, n_cols)),
+            sem((n_ep, n_cols)),
             sem((n_ep, n_seq)),
             sem((n_ep, n_seq)),
             sem((n_ep,)),
-            sem((n_ep, n_seq)),
-            sem((n_ep, n_seq)),
-            sem((n_ep,)),
-            sem((n_ep, len(column_chunks(width)))),
-            sem((n_ep + 1, len(column_chunks(width)))),
+            sem((n_ep, n_cols)),
+            sem((n_ep + 1, n_cols)),
         ],
         compiler_params=pltpu.CompilerParams(
-            collective_id=1, has_side_effects=True, vmem_limit_bytes=64000 << 10
+            collective_id=1, has_side_effects=True, vmem_limit_bytes=65200 << 10
         ),
         name="mixture",
-    )(rows_in, picks, gates, mixed, w_in, w_out)
+    )(attended, out_rows, own, gain, picks, gates, w_in, w_out)
 
 
 def slot_of(ids, capacity):
@@ -729,14 +886,6 @@
     attended = lax.map(one_block, jnp.arange(tok_rows // block_len, dtype=jnp.int32)).reshape(
         tok_rows, q_cols
     )
-    head_partial = lax.dot_general(
-        attended, out_rows, (((1,), (1,)), ((), ())), preferred_element_type=jnp.float32
-    ).astype(jnp.bfloat16)
-    head_sum = lax.psum_scatter(
-        by_rows(head_partial), "ep", scatter_dimension=0, tiled=True
-    ).astype(jnp.float32)
-    mixed = act_f32 + head_sum
-    mlp_in = normed(mixed, mlp_gain).astype(jnp.bfloat16)
     plane_rows = seq_count * capacity
     place = jnp.arange(plane_rows, dtype=jnp.int32)
     first_slots = (place // capacity * ep_count + lax.axis_index("ep")) * capacity
@@ -755,7 +904,15 @@
     )
     gate_parts = jnp.concatenate(three_parts(gate_at), axis=1)
     return mixture(
-        mlp_in, picks, gate_parts, mixed, expert_in[0], expert_out[0], capacity
+        attended,
+        out_rows,
+        activations,
+        mlp_gain[None, :],
+        picks,
+        gate_parts,
+        expert_in[0],
+        expert_out[0],
+        capacity,
     )
 
 

time: 349 us -> 332 us (0.951)
  Pallas kernels: 212 us -> 274 us
  waiting for transfers between devices: 55.1 us -> 0.01 us
  between operations: 14.1 us -> 0.72 us
  matrix products: 26.4 us -> 18.5 us
  other arithmetic: 15.7 us -> 10.6 us
    pallas_call x1, Pallas kernels: 150 us -> 213 us  [mixture(): pl.pallas_call(functools.partial(layer_kernel, n_seq, n_ep, cap), out_sha...]
    reduce_scatter x1 -> x0, waiting for transfers between devices: 55 us -> none  [body(): lax.psum_scatter(by_rows(head_partial), 'ep', scatter_dimension=0, tiled=...]
    dot_general x1 -> x0, matrix products: 6.11 us -> none  [body(): lax.dot_general(attended, out_rows, (((1,), (1,)), ((), ())), preferred_e...]
    unnamed x36 -> x24, local copies, waits for them, and re-layouts: 11.2 us -> 12.9 us
  transfers between devices with their start and end apart: 3 -> 2, of which waited for: 1 -> 0; matrix products, arithmetic and copies ran while one was open for 4% -> 4% of each run, Pallas kernels for 0% -> 0%
where the time goes in v4:
time: 332 us; the launch traced here: 328 us
  Pallas kernels  274 us (83%)
  matrix products  18.5 us (6%)
  local copies, waits for them, and re-layouts  17.6 us (5%)
  other arithmetic  10.6 us (3%)
  starting transfers between devices  6.08 us (2%)
    pallas_call x1, Pallas kernels, mixture(): pl.pallas_call(functools.partial(layer_kernel, n_seq, n_ep, cap), out_sha...  213 us
    pallas_call x1, Pallas kernels, gathered(): pl.pallas_call(functools.partial(gather_kernel, n_seq, n_ep, n_line, n_pl...  61.8 us
    unnamed x24, local copies, waits for them, and re-layouts  12.9 us
    another operation x2, matrix products, by_rows(): return with_layout_constraint(x, Layout(tuple(range(x.ndim))))  7.79 us
  transfers between devices with their start and end apart: 2, of which 0 were waited for; matrix products, arithmetic and copies ran while one was open for 4% of the time, Pallas kernels for 0%

profile of v4, /device:TPU:0, one launch (start us, length us, event | category | flops | bytes accessed | tf_op | source)
XLA Modules:
  0.0 328.1 jit_solution(17144429011250087247)
XLA Ops:
  0.0 1.5 copy.35.rows_ref
  1.7 0.8 copy.36
  3.8 0.9 fusion.5.refs_0_
  4.7 1.1 copy-done.1
  5.8 1.1 copy-done.2
  7.0 0.9 copy-done.4
  7.9 0.9 copy-done.5
  9.4 61.8 %gather.1 = (bf16[4,128,2880]{2,1,0:T(8,128)(2,1)S(1)}, s32[4,4,128]{2,1,0:T(4,128)S(1)}, f32[4,4,128]{2,1,0:T(4,128)S(1)}, bf16[8,360,1024]{2,1,0:T(8,128)(2,1)...) custom-call(bf16[128,2880]{1,0:T(8,128)(2,1)S(1)} %fusion.5.refs_0_, ...), custom_call_target="tpu_custom_call" | custom-call | tf_op jit(solution)/shard_map/gather/pallas_call | solution.py:245
  71.3 2.5 copy-done
  73.8 0.9 copy-done.3
  74.7 2.6 copy-done.7
  77.2 0.9 convolution_convert_fusion
  78.2 2.4 collective-permute-start
  80.6 2.2 fusion.34
  83.2 3.7 %collective-permute-start.1 = (bf16[128,128]{0,1:T(8,128)(2,1)S(1)}, bf16[128,128]{0,1:T(8,128)(2,1)}, u32[]{:S(2)}, u32[]{:S(2)}) collective-permute-start(bf16[128,128]{0,1:T(8,128)(2,1)S(1)} %bitcast.75), channel_id=1, source_target_pairs={{0,4},{4,8},{8,12},{12,16},{16,20},{20,24},{24,28},{1,5},{5,9},{9,... | collective-permute-start | bytes 98312 | tf_op jit(solution)/shard_map/ppermute | solution.py:20
  87.0 5.5 %fusion.35 = f32[512,1024]{0,1:T(8,128)S(1)} fusion(bf16[512,2880]{1,0:T(8,128)(2,1)S(1)} %bitcast.61, bf16[2880,1024]{1,0:T(8,128)(2,1)} %bitcast.65), kind=kOutput, calls=%fused_computation.77 | convolution fusion | flops 3019898880 | bytes 10944512 | tf_op jit(solution)/shard_map/layout_constraint | solution.py:813
  93.4 0.9 fusion.17.pick_ref
  95.0 1.0 pad_maximum_fusion.gate_ref
  96.9 3.9 %fusion.1 = (f32[2,8,512]{2,1,0:T(8,128)S(1)}, f32[2,640,512,8]{2,1,3,0:T(8,128)S(1)}) fusion(pred[512,640]{0,1:T(8,128)(4,1)S(1)} %fusion.8, bf16[512,2,8,32]{0,3,2,1:T(8,128)(2,1)S(1)} %bitcast.73, bf16[512,2,8,32]{0,3,2,1:T(8,128)(2,1)S(1)} %bitcast.72, bf16[512,2,32]{0,2,1:T(8,128)(2,1)S(1)} %get-tuple-element.43, ...), kind=kOutput, calls=%fused_computation.4 | convolution fusion | flops 689397760 | bytes 22544384 | tf_op jit(solution)/shard_map/while/body/eval_jaxpr/qkgd,jkd->kgqj/dot_general | solution.py:43
  100.9 4.5 %fusion = f32[2,8,512]{2,1,0:T(8,128)S(1)} fusion(f32[2,640,512,8]{2,1,3,0:T(8,128)S(1)} %get-tuple-element.58, f32[2,8,512]{2,1,0:T(8,128)S(1)} %broadcast_maximum_fusion, pred[512,640]{0,1:T(8,128)(4,1)S(1)} %fusion.8), kind=kLoop, calls=%fused_computation.3 | loop fusion | flops 20963328 | bytes 21364736 | tf_op jit(solution)/shard_map/while/body/eval_jaxpr/reduce_sum | solution.py:52
  105.5 5.9 %fusion.6 = bf16[2,64,8,512]{3,1,2,0:T(8,128)(2,1)S(1)} fusion(bf16[640,2,64,1]{0,2,3,1:T(8,128)(2,1)S(1)} %bitcast.74, f32[2,640,512,8]{2,1,3,0:T(8,128)S(1)} %get-tuple-element.58, f32[2,8,512]{2,1,0:T(8,128)S(1)} %exponential_add_fusion, f32[2,8,512]{2,1,0:T(8,128)S(1)} %broadcast_maximum_fusion, pred[512,640]{0,1:T(8,128)(4,1)S(1)} %fusion.8), kind=kOutput, calls=%fused_computation.13 | convolution fusion | flops 697827328 | bytes 22577152 | tf_op jit(solution)/shard_map/while/body/eval_jaxpr/kgqj,jkd->qkgd/dot_general | solution.py:54
  111.4 1.3 copy.42.att_ref
  112.8 212.6 %mixture.1 = bf16[128,2880]{1,0:T(8,128)(2,1)} custom-call(bf16[512,1024]{1,0:T(8,128)(2,1)} %copy.42.att_ref, bf16[2880,1024]{1,0:T(8,128)(2,1)} %bitcast.58, bf16[128,2880]{1,0:T(8,128)(2,1)} %copy-done.8, f32[1,2880]{1,0:T(1,128)} %broadcast_in_dim.86.gain_ref, bf16[4,192,128]{2,1,0:T(8,128)(2,1)} %fusion.17.pick_ref, ...), custom_call_target="tpu_custom_call" | custom-call | tf_op jit(solution)/shard_map/mixture/pallas_call | solution.py:755
  325.4 2.3 copy.44
  (45 shorter events, 5.1 us)
Async XLA Ops:
  1.5 3.3 copy-start.8
  4.7 1.1 copy-start.1
  5.8 1.1 copy-start.2
  7.0 0.9 copy-start.4
  7.9 0.9 copy-start.5
  8.7 0.7 copy-start.6
  71.3 2.5 copy-start
  73.8 0.9 copy-start.3
  74.7 2.6 copy-start.7
  78.2 18.5 %collective-permute-start = (bf16[128,128]{1,0:T(8,128)(2,1)S(1)}, bf16[128,128]{1,0:T(8,128)(2,1)S(1)}, u32[]{:S(2)}, u32[]{:S(2)}) collective-permute-start(bf16[128,128]{1,0:T(8,128)(2,1)S(1)} %slice.64), channel_id=1, source_target_pairs={{0,4},{4,8},{8,12},{12,16},{16,20},{20,24},{24,28},{1,5},{5,9},{9,... | collective-permute-start | bytes 98312 | tf_op jit(solution)/shard_map/ppermute | solution.py:20
  83.2 13.7 %collective-permute-start.1 = (bf16[128,128]{0,1:T(8,128)(2,1)S(1)}, bf16[128,128]{0,1:T(8,128)(2,1)}, u32[]{:S(2)}, u32[]{:S(2)}) collective-permute-start(bf16[128,128]{0,1:T(8,128)(2,1)S(1)} %bitcast.75), channel_id=1, source_target_pairs={{0,4},{4,8},{8,12},{12,16},{16,20},{20,24},{24,28},{1,5},{5,9},{9,... | collective-permute-start | bytes 98312 | tf_op jit(solution)/shard_map/ppermute | solution.py:20
  92.5 3.5 %copy-start.10 = (f32[16]{0:T(128)S(1)}, f32[16]{0:T(128)}, u32[]{:S(2)}) copy-start(f32[16]{0:T(128)} %param.18) | copy-start | bytes 196
  92.5 3.6 %copy-start.9 = (f32[2880]{0:T(1024)S(1)}, f32[2880]{0:T(1024)}, u32[]{:S(2)}) copy-start(f32[2880]{0:T(1024)} %param.19) | copy-start | bytes 34564

commit v5 on v4

--- a/solution.py
+++ b/solution.py
@@ -26,33 +26,78 @@
 
 
 def rotate(head_vals, positions):
-    half_dim = head_vals.shape[-1] // 2
+    half_dim = head_vals.shape[1] // 2
     inv_freq = 150000.0 ** (-jnp.arange(half_dim, dtype=jnp.float32) / half_dim)
-    angles = positions[:, None] * inv_freq[None, :]
-    cosines = jnp.cos(angles)[:, None, :]
-    sines = jnp.sin(angles)[:, None, :]
-    first = head_vals[..., :half_dim]
-    second = head_vals[..., half_dim:]
+    angles = inv_freq[:, None] * positions[None, :]
+    cosines = jnp.cos(angles)[None]
+    sines = jnp.sin(angles)[None]
+    first = head_vals[:, :half_dim]
+    second = head_vals[:, half_dim:]
     return jnp.concatenate(
-        [first * cosines - second * sines, second * cosines + first * sines], axis=-1
+        [first * cosines - second * sines, second * cosines + first * sines], axis=1
     )
 
 
-def attend(queries, key_rows, val_rows, sink_grid, query_first, win_len):
-    scores = (
-        jnp.einsum("qkgd,jkd->kgqj", queries, key_rows, preferred_element_type=jnp.float32) * 0.125
-    )
-    q_pos = query_first + jnp.arange(queries.shape[0], dtype=jnp.int32)
-    k_pos = query_first - win_len + jnp.arange(key_rows.shape[0], dtype=jnp.int32)
-    offset = q_pos[:, None] - k_pos[None, :]
-    allowed = (offset >= 0) & (offset < win_len) & (k_pos[None, :] >= 0)
-    scores = jnp.where(allowed, scores, jnp.float32(-1e30))
-    peak_val = jnp.maximum(jnp.max(scores, axis=-1), sink_grid[:, :, None])
-    exp_terms = jnp.exp(scores - peak_val[..., None])
-    denominator = jnp.sum(exp_terms, axis=-1) + jnp.exp(sink_grid[:, :, None] - peak_val)
-    weights = (exp_terms / denominator[..., None]).astype(jnp.bfloat16)
-    mixed_vals = jnp.einsum("kgqj,jkd->qkgd", weights, val_rows, preferred_element_type=jnp.float32)
-    return mixed_vals.astype(jnp.bfloat16)
+def attend_kernel(heads, q_ref, key_ref, val_ref, sink_ref, out_ref):
+    tokens = q_ref.shape[1]
+    first_pos = lax.axis_index("seq") * tokens
+    groups = key_ref.shape[0] // HD
+    lanes = heads * WIN
+
+    @pl.loop(0, tokens // WIN)
+    def _(block):
+        start = pl.multiple_of(block * WIN, WIN)
+        key_at = lax.broadcasted_iota(jnp.int32, (2 * WIN, WIN), 0)
+        query_at = lax.broadcasted_iota(jnp.int32, (2 * WIN, WIN), 1)
+        offset = WIN + query_at - key_at
+        inside = first_pos + start - WIN + key_at >= 0
+        allowed = (offset >= 0) & (offset < WIN) & inside
+        barred = jnp.where(allowed, 0.0, jnp.float32(-1e30))
+        for g in range(groups):
+            first = g * heads * HD
+            queries = jnp.concatenate(
+                [
+                    q_ref[first + h * HD : first + (h + 1) * HD, pl.ds(start, WIN)]
+                    for h in range(heads)
+                ],
+                axis=1,
+            )
+            keys = key_ref[g * HD : (g + 1) * HD, pl.ds(start, 2 * WIN)]
+            values = val_ref[g * HD : (g + 1) * HD, pl.ds(start, 2 * WIN)]
+            scores = lax.dot_general(
+                keys, queries, (((0,), (0,)), ((), ())), preferred_element_type=jnp.float32
+            )
+            bars = jnp.concatenate([barred] * heads, axis=1)
+            scores = jnp.where(bars < 0.0, bars, scores * 0.125)
+            sink = sink_ref[g : g + 1, :]
+            peak = jnp.maximum(jnp.max(scores, axis=0, keepdims=True), sink)
+            terms = jnp.exp(scores - peak)
+            total = jnp.sum(terms, axis=0, keepdims=True) + jnp.exp(sink - peak)
+            weights = (terms * (1.0 / total)).astype(jnp.bfloat16)
+            mixed = jnp.dot(values, weights, preferred_element_type=jnp.float32)
+            for h in range(0, heads, 2):
+                pair = jnp.concatenate(
+                    [mixed[:, h * WIN : (h + 1) * WIN], mixed[:, (h + 1) * WIN : (h + 2) * WIN]],
+                    axis=0,
+                )
+                at = first + h * HD
+                out_ref[pl.ds(start, WIN), at : at + 2 * HD] = pair.T.astype(jnp.bfloat16)
+
+
+def attend(queries, keys, values, sinks, heads):
+    cols, tokens = queries.shape
+    vmem = pl.BlockSpec(memory_space=pltpu.VMEM)
+    return pl.pallas_call(
+        functools.partial(attend_kernel, heads),
+        out_shape=jax.ShapeDtypeStruct((tokens, cols), jnp.bfloat16),
+        in_specs=[vmem] * 4,
+        out_specs=vmem,
+        compiler_params=pltpu.CompilerParams(vmem_limit_bytes=24 << 20),
+        cost_estimate=pl.CostEstimate(
+            flops=8 * cols * tokens * WIN, bytes_accessed=4 * cols * tokens, transcendentals=0
+        ),
+        name="attend",
+    )(queries, keys, values, jnp.repeat(sinks, WIN, axis=1))
 
 
 def remote(src, dst, send_sem, recv_sem, device):
@@ -259,7 +304,7 @@
             sem((n_plane, n_seq)),
         ],
         compiler_params=pltpu.CompilerParams(
-            collective_id=0, has_side_effects=True, vmem_limit_bytes=16 << 20
+            collective_id=0, has_side_effects=True, vmem_limit_bytes=60 << 20
         ),
         name="gather",
     )(*arrays)
@@ -846,45 +891,30 @@
     )
     normed_all = normed_all.reshape(tok_rows, width_dim)
     *shard_rows, out_rows = [rows.reshape(width_dim, -1) for rows in shard_rows]
-    q_lin, k_lin, v_lin = tuple(
-        (
-            jnp.dot(normed_all, weight_rows, preferred_element_type=jnp.float32)
-            for weight_rows in shard_rows
-        )
-    )
-    q_lin, k_lin = by_rows(q_lin), by_rows(k_lin)
+
+    def projected(weight_rows):
+        return by_rows(jnp.dot(normed_all, weight_rows, preferred_element_type=jnp.float32)).T
+
+    q_lin, k_lin, v_lin = [projected(weight_rows) for weight_rows in shard_rows]
     first_pos = lax.axis_index("seq") * tok_rows
     positions = (first_pos + jnp.arange(tok_rows, dtype=jnp.int32)).astype(jnp.float32)
     q_heads = q_cols // HD
     kv_heads = kv_cols // HD
     group_size = q_heads // kv_heads
-    queries = (
-        rotate(q_lin.reshape(tok_rows, q_heads, HD), positions)
-        .astype(jnp.bfloat16)
-        .reshape(tok_rows, kv_heads, group_size, HD)
-    )
-    keys_rot = (
-        rotate(k_lin.reshape(tok_rows, kv_heads, HD), positions)
-        .astype(jnp.bfloat16)
-        .reshape(tok_rows, kv_cols)
-    )
-    values_cast = v_lin.astype(jnp.bfloat16)
-    prev_keys, prev_values = passed_along(
-        (keys_rot[tok_rows - WIN :], values_cast[tok_rows - WIN :]), "seq", 1
-    )
-    key_all = jnp.concatenate([prev_keys, keys_rot], axis=0).reshape(WIN + tok_rows, kv_heads, HD)
-    val_all = jnp.concatenate([prev_values, values_cast], axis=0).reshape(
-        WIN + tok_rows, kv_heads, HD
-    )
-    block_len = min(tok_rows, 512)
-    sink_grid = sink_logits.reshape(kv_heads, group_size)
-
-    def one_block(block):
-        row_first = block * block_len
-        return attend(queries, key_all, val_all, sink_grid, first_pos + row_first, WIN)
-
-    attended = lax.map(one_block, jnp.arange(tok_rows // block_len, dtype=jnp.int32)).reshape(
-        tok_rows, q_cols
+
+    def rotated(lin):
+        heads = lin.reshape(-1, HD, tok_rows)
+        return rotate(heads, positions).astype(jnp.bfloat16).reshape(lin.shape)
+
+    keys_values = jnp.concatenate([rotated(k_lin), v_lin.astype(jnp.bfloat16)], axis=0)
+    before = passed_along(keys_values[:, tok_rows - WIN :], "seq", 1)
+    keys_values = jnp.concatenate([before, keys_values], axis=1)
+    attended = attend(
+        rotated(q_lin),
+        keys_values[:kv_cols],
+        keys_values[kv_cols:],
+        sink_logits.reshape(kv_heads, group_size),
+        group_size,
     )
     plane_rows = seq_count * capacity
     place = jnp.arange(plane_rows, dtype=jnp.int32)

time: 332 us -> 318 us (0.958)
  Pallas kernels: 274 us -> 285 us
  local copies, waits for them, and re-layouts: 17.6 us -> 10.3 us
  matrix products: 18.5 us -> 11.8 us
  starting transfers between devices: 6.08 us -> 2.35 us
    unnamed x24 -> x20, local copies, waits for them, and re-layouts: 12.9 us -> 3.67 us
    pallas_call x0 -> x1, Pallas kernels: none -> 5.32 us  [attend(): pl.pallas_call(functools.partial(attend_kernel, heads), out_shape=jax.Sha...]
    pallas_call x1, Pallas kernels: 213 us -> 217 us  [mixture(): pl.pallas_call(functools.partial(layer_kernel, n_seq, n_ep, cap), out_sha...]
    reduce_sum x1 -> x0, other arithmetic: 4.54 us -> none  [attend(): jnp.sum(exp_terms, axis=-1) + jnp.exp(sink_grid[:, :, None] - peak_val)]
    another operation x2 -> x1, matrix products: 7.79 us -> 3.3 us  [by_rows(): return with_layout_constraint(x, Layout(tuple(range(x.ndim))))]
    ppermute x2 -> x1, starting transfers between devices: 6.08 us -> 2.35 us  [passed_along(): return lax.ppermute(x, axis, pairs)]
    dot_general x3 -> x2, matrix products: 10.8 us -> 8.46 us  [projected(): jnp.dot(normed_all, weight_rows, preferred_element_type=jnp.float32)]
  transfers between devices with their start and end apart: 2 -> 1, of which waited for: 0 -> 0; matrix products, arithmetic and copies ran while one was open for 4% -> 4% of each run, Pallas kernels for 0% -> 0%
where the time goes in v5:
time: 318 us; the launch traced here: 317 us
  Pallas kernels  285 us (90%)
  matrix products  11.8 us (4%)
  local copies, waits for them, and re-layouts  10.3 us (3%)
  other arithmetic  7.37 us (2%)
    pallas_call x1, Pallas kernels, mixture(): pl.pallas_call(functools.partial(layer_kernel, n_seq, n_ep, cap), out_sha...  217 us
    pallas_call x1, Pallas kernels, gathered(): pl.pallas_call(functools.partial(gather_kernel, n_seq, n_ep, n_line, n_pl...  62.5 us
    dot_general x2, matrix products, projected(): jnp.dot(normed_all, weight_rows, preferred_element_type=jnp.float32)  8.46 us
  transfers between devices with their start and end apart: 1, of which 0 were waited for; matrix products, arithmetic and copies ran while one was open for 4% of the time, Pallas kernels for 0%

profile of v5, /device:TPU:0, one launch (start us, length us, event | category | flops | bytes accessed | tf_op | source)
XLA Modules:
  0.0 317.2 jit_solution(17245416647123348941)
XLA Ops:
  0.0 0.8 copy.30
  1.4 1.3 add_bitcast_fusion.refs_1_
  2.6 1.5 copy.29.rows_ref
  4.4 1.1 fusion.2.refs_0_
  5.5 62.5 %gather.1 = (bf16[4,128,2880]{2,1,0:T(8,128)(2,1)}, s32[4,4,128]{2,1,0:T(4,128)}, f32[4,4,128]{2,1,0:T(4,128)}, bf16[8,360,1024]{2,1,0:T(8,128)(2,1)}, bf16[8,36...) custom-call(bf16[128,2880]{1,0:T(8,128)(2,1)} %fusion.2.refs_0_, ...), custom_call_target="tpu_custom_call" | custom-call | tf_op jit(solution)/shard_map/gather/pallas_call | solution.py:290
  68.0 3.3 %fusion.3 = bf16[128,512]{1,0:T(8,128)(2,1)S(1)} fusion(bf16[512,2880]{1,0:T(8,128)(2,1)} %bitcast.42, bf16[2880,128]{1,0:T(8,128)(2,1)} %bitcast.54), kind=kOutput, calls=%fused_computation.8 | convolution fusion | flops 377552896 | bytes 3817472 | tf_op jit(solution)/shard_map/layout_constraint | solution.py:858
  71.4 1.0 convolution_bitcast_fusion.1
  72.3 0.8 copy.33
  73.1 0.3 multiply_cosine_fusion
  73.5 1.0 subtract_convert_fusion.1
  74.5 2.4 collective-permute-start
  76.9 0.7 reshape.169
  77.7 7.5 %convolution_bitcast_fusion = f32[1024,512]{0,1:T(8,128)} fusion(bf16[512,2880]{1,0:T(8,128)(2,1)S(1)} %bitcast.44, bf16[2880,1024]{1,0:T(8,128)(2,1)} %bitcast.68), kind=kOutput, calls=%fused_computation.2 | convolution fusion | flops 3019898880 | bytes 10944512 | tf_op jit(solution)/shard_map/dot_general | solution.py:896
  85.2 1.9 copy.32
  87.2 0.3 subtract_convert_fusion
  87.5 0.3 copy-done.7
  88.0 0.9 fusion.8.pick_ref
  88.9 0.7 reduce-precision_convert_fusion.1
  89.6 1.0 pad_maximum_fusion.1.gate_ref
  90.6 0.6 broadcast_in_dim.65.gain_ref
  91.3 5.3 %attend.1.att_ref = bf16[512,1024]{1,0:T(8,128)(2,1)S(1)} custom-call(bf16[1024,512]{1,0:T(8,128)(2,1)S(1)} %bitcast.40, bf16[128,640]{1,0:T(8,128)(2,1)S(1)} %get-tuple-element.24.key_ref, bf16[128,640]{1,0:T(8,128)(2,1)S(1)} %get-tuple-element.23.val_ref, f32[2,1024]{1,0:T(2,128)S(1)} %bitcast.41), custom_call_target="tpu_custom_call" | custom-call | flops 536870912 | bytes 2097152 | tf_op jit(solution)/shard_map/attend/pallas_call | solution.py:90
  96.6 1.0 copy-done
  97.6 217.3 %mixture.1 = bf16[128,2880]{1,0:T(8,128)(2,1)} custom-call(bf16[512,1024]{1,0:T(8,128)(2,1)} %copy-done, bf16[2880,1024]{1,0:T(8,128)(2,1)} %bitcast.48, bf16[128,2880]{1,0:T(8,128)(2,1)} %copy-done.2, f32[1,2880]{1,0:T(1,128)} %broadcast_in_dim.65.gain_ref, bf16[4,192,128]{2,1,0:T(8,128)(2,1)} %fusion.8.pick_ref, ...), custom_call_target="tpu_custom_call" | custom-call | tf_op jit(solution)/shard_map/mixture/pallas_call | solution.py:800
  315.0 2.3 copy.36
  (33 shorter events, 1.1 us)
Async XLA Ops:
  0.0 4.4 %copy-start.4 = (f32[2880]{0:T(1024)S(1)}, f32[2880]{0:T(1024)}, u32[]{:S(2)}) copy-start(f32[2880]{0:T(1024)} %param.13) | copy-start | bytes 34564
  4.1 1.4 copy-start.2
  68.0 3.3 %copy-start.1 = (bf16[4,128,2880]{2,1,0:T(8,128)(2,1)S(1)}, bf16[4,128,2880]{2,1,0:T(8,128)(2,1)}, u32[]{:S(2)}) copy-start(bf16[4,128,2880]{2,1,0:T(8,128)(2,1)} %get-tuple-element.12) | copy-start | bytes 8847364
  68.0 3.3 %copy-start.3 = (bf16[8,360,128]{2,1,0:T(8,128)(2,1)S(1)}, bf16[8,360,128]{2,1,0:T(8,128)(2,1)}, u32[]{:S(2)}) copy-start(bf16[8,360,128]{2,1,0:T(8,128)(2,1)} %get-tuple-element.14) | copy-start | bytes 2211844
  74.5 16.7 %collective-permute-start = (bf16[256,128]{1,0:T(8,128)(2,1)S(1)}, bf16[256,128]{1,0:T(8,128)(2,1)S(1)}, u32[]{:S(2)}, u32[]{:S(2)}) collective-permute-start(bf16[256,128]{1,0:T(8,128)(2,1)S(1)} %pad_maximum_fusion.3), channel_id=1, source_target_pairs={{0,4},{4,8},{8,12},{12,16},{16,20},{20,24},{24,28},{1,5},{5,9},{9,... | collective-permute-start | bytes 196616 | tf_op jit(solution)/shard_map/ppermute | solution.py:20
  87.1 0.7 copy-start.7
  87.2 0.7 copy-start.6
  87.9 2.7 copy-start.5
  96.6 1.0 copy-start
